TPU v7x, 32 devices: a whole 2x2x4 slice. The times are simulated.
32 devices in a mesh: seq: 16 (over z, y, core), head: 2 (over x).
Axes of the slice: x: 2, y: 2, z: 4, core: 2. Of those that a mesh axis runs over, the one named last changes fastest.
Arguments:
- query_in: bfloat16 [6144, 512], P('seq', 'head'), may hold values from -6 to 6
- key_in: bfloat16 [6144, 512], P('seq', 'head'), may hold values from -6 to 6
- value_in: bfloat16 [6144, 512], P('seq', 'head'), may hold values from -6 to 6
- text_keys: bfloat16 [256, 512], P(None, 'head'), may hold values from -6 to 6
- text_values: bfloat16 [256, 512], P(None, 'head'), may hold values from -6 to 6
- text_mask: int32 [256], replicated, may hold values 0 or 1
- window_reach: int32 [4, 2], P('head'), may hold values from 0 to 1
- tile_map: int32 [16, 3], replicated, may hold values from 0 to 14, as said below
- out_weight: bfloat16 [512, 3072], P('head'), may hold values from -0.25 to 0.25
- gate_scale: float32 [3072], replicated, may hold values from -4 to 4
- grad_out: bfloat16 [6144, 3072], P('seq', 'head'), may hold values from -12 to 12
Outputs:
- grad_query: bfloat16 [6144, 512], P('seq', 'head')
- grad_key: bfloat16 [6144, 512], P('seq', 'head')
- grad_value: bfloat16 [6144, 512], P('seq', 'head')
- grad_text_keys: bfloat16 [256, 512], P(None, 'head')
- grad_text_values: bfloat16 [256, 512], P(None, 'head')
- grad_gate: float32 [3072], replicated
Inputs may be any that keep to these rules, and one draw needn't show every extreme that they name: `tile_map`: index i of seq sits at grid row i // 8 and grid column i % 8. Its tile row is that grid row, or 1 minus it, plus an offset; its tile column is the grid column, or 7 minus it, plus an offset; the mirroring and the offsets are the same for all indices, and so is the frame coordinate. Of the two offsets, the one of the longer grid dimension (rows when they are equal) is 7, the other 0.
All inputs are finite; a program needn't handle non-finite values.
Results may differ from a plain program's by a relative error of at most 0.02035.
The roundings to bfloat16 on the way count: a program that leaves them out, or rounds other values in their place, can miss the bound.
Values may be sent and summed in bfloat16 or wider, within the bound.
A program may use at most 64 MiB of HBM per device.

v0:
```python
import jax
import jax.numpy as jnp
import numpy as np
from jax import lax
from jax.sharding import PartitionSpec as P

HEAD_DIM = 128
TILE_T = 6
TILE_H = 8
TILE_W = 8
COLS = 8


theta_base = 256.0


def from_behind(array, axis, by):
    length = lax.axis_size(axis)
    pairs = [(i, i + by) for i in range(length) if 0 <= i + by < length]
    return lax.ppermute(array, axis, pairs)


def sections(head_dim):
    first = head_dim // 8
    second = (head_dim - first) // 2
    return ((0, first), (first, second), (first + second, second))


def rotate(values, frame_pos, row_pos, col_pos, direction):
    pieces = []
    for (offset, length), where_pos in zip(
        sections(values.shape[-1]), (frame_pos, row_pos, col_pos)
    ):
        half_len = length // 2
        freqs = theta_base ** (-2.0 * jnp.arange(half_len, dtype=jnp.float32) / length)
        angles = where_pos.astype(jnp.float32)[:, None] * freqs[None, :]
        cosine = jnp.cos(angles)[:, None, :]
        sine_part = jnp.sin(angles)[:, None, :]
        first_half = values[..., offset : offset + half_len]
        second_half = values[..., offset + half_len : offset + length]
        pieces.append(first_half * cosine - direction * second_half * sine_part)
        pieces.append(direction * first_half * sine_part + second_half * cosine)
    return jnp.concatenate(pieces, axis=-1)


def local_positions(tile_coords):
    local_index = jnp.arange(TILE_T * TILE_H * TILE_W, dtype=jnp.int32)
    plane_size = TILE_H * TILE_W
    frame_pos = tile_coords[:, 0:1] * TILE_T + (local_index // plane_size)[None, :]
    row_pos = tile_coords[:, 1:2] * TILE_H + (local_index // TILE_W % TILE_H)[None, :]
    col_pos = tile_coords[:, 2:3] * TILE_W + (local_index % TILE_W)[None, :]
    return (frame_pos.reshape(-1), row_pos.reshape(-1), col_pos.reshape(-1))


def head_scores(queries, key_block, score_scale):
    return (
        jnp.einsum("qhd,khd->hqk", queries, key_block, preferred_element_type=jnp.float32)
        * score_scale
    )


def merge_stats(running_max, running_sum, scores):
    new_max = jnp.maximum(running_max, jnp.max(scores, axis=-1))
    new_sum = running_sum * jnp.exp(running_max - new_max) + jnp.sum(
        jnp.exp(scores - new_max[..., None]), axis=-1
    )
    return (new_max, new_sum)


def on_device(
    query_in,
    key_in,
    value_in,
    text_keys,
    text_values,
    text_mask,
    window_reach,
    tile_map,
    out_weight,
    gate_scale,
    grad_out,
):
    tile_rows = query_in.shape[0]
    feature_width = query_in.shape[1]
    head_count = feature_width // HEAD_DIM
    text_count = text_keys.shape[0]
    row_count = lax.axis_size("seq") // COLS
    device = lax.axis_index("seq")
    score_scale = HEAD_DIM ** (-0.5)
    split_shape = (tile_rows, head_count, HEAD_DIM)
    own_coords = tile_map[device]
    frame_pos, row_pos, col_pos = local_positions(own_coords[None, :])
    queries = rotate(
        query_in.astype(jnp.float32).reshape(split_shape), frame_pos, row_pos, col_pos, 1.0
    ).astype(jnp.bfloat16)
    keys_rot = rotate(
        key_in.astype(jnp.float32).reshape(split_shape), frame_pos, row_pos, col_pos, 1.0
    ).astype(jnp.bfloat16)
    packed = jnp.stack([keys_rot.reshape(tile_rows, feature_width), value_in])
    row_steps = np.array([-1, -1, -1, 0, 0, 0, 1, 1, 1], dtype=np.int32)
    col_steps = np.array([-1, 0, 1, -1, 0, 1, -1, 0, 1], dtype=np.int32)
    fetched = []
    for number in range(9):
        if number == 4:
            fetched.append(packed)
        else:
            fetched.append(
                from_behind(packed, "seq", int(row_steps[number]) * COLS + int(col_steps[number]))
            )
    blocks = jnp.stack(fetched)
    source_row = device // COLS - jnp.asarray(row_steps)
    source_col = device % COLS - jnp.asarray(col_steps)
    usable_block = (
        (source_row >= 0) & (source_row < row_count) & (source_col >= 0) & (source_col < COLS)
    )
    source = jnp.clip(source_row, 0, row_count - 1) * COLS + jnp.clip(source_col, 0, COLS - 1)
    near_coords = tile_map[source]
    row_gap = jnp.abs(near_coords[:, 1] - own_coords[1])
    col_gap = jnp.abs(near_coords[:, 2] - own_coords[2])
    allowed = (
        usable_block[None, :]
        & (row_gap[None, :] <= window_reach[:, 0:1])
        & (col_gap[None, :] <= window_reach[:, 1:2])
    )
    allow_rows = allowed.T
    text_open = (text_mask == 1)[None, None, :]
    block_keys = blocks[:, 0].reshape(9, tile_rows, head_count, HEAD_DIM)
    block_values = blocks[:, 1].reshape(9, tile_rows, head_count, HEAD_DIM)
    text_key_split = text_keys.reshape(text_count, head_count, HEAD_DIM)
    text_value_split = text_values.reshape(text_count, head_count, HEAD_DIM)

    def stats_step(carry, inputs):
        key_block, allow = inputs
        scores = jnp.where(
            allow[:, None, None], head_scores(queries, key_block, score_scale), -jnp.inf
        )
        return (merge_stats(carry[0], carry[1], scores), None)

    start_stats = (
        jnp.full((head_count, tile_rows), -1e30, jnp.float32),
        jnp.zeros((head_count, tile_rows), jnp.float32),
    )
    (running_max, running_sum), _ = lax.scan(stats_step, start_stats, (block_keys, allow_rows))
    text_scores = jnp.where(text_open, head_scores(queries, text_key_split, score_scale), -jnp.inf)
    running_max, running_sum = merge_stats(running_max, running_sum, text_scores)
    log_norm = running_max + jnp.log(running_sum)

    def weights_for(key_block, allow_mask):
        scores = head_scores(queries, key_block, score_scale)
        return jnp.where(allow_mask, jnp.exp(scores - log_norm[:, :, None]), 0.0)

    def output_step(total_out, inputs):
        key_block, value_block, allow = inputs
        probs = weights_for(key_block, allow[:, None, None]).astype(jnp.bfloat16)
        return (
            total_out
            + jnp.einsum("hqk,khd->hqd", probs, value_block, preferred_element_type=jnp.float32),
            None,
        )

    total_out, _ = lax.scan(
        output_step,
        jnp.zeros((head_count, tile_rows, HEAD_DIM), jnp.float32),
        (block_keys, block_values, allow_rows),
    )
    text_probs = weights_for(text_key_split, text_open).astype(jnp.bfloat16)
    total_out = total_out + jnp.einsum(
        "hqk,khd->hqd", text_probs, text_value_split, preferred_element_type=jnp.float32
    )
    attn = total_out.transpose(1, 0, 2).reshape(tile_rows, feature_width).astype(jnp.bfloat16)
    piece = lax.all_gather(grad_out, "head", axis=1, tiled=True)
    grad_proj = (piece.astype(jnp.float32) * gate_scale[None, :]).astype(jnp.bfloat16)
    grad_acc = lax.dot_general(
        grad_proj, out_weight, (((1,), (1,)), ((), ())), preferred_element_type=jnp.float32
    )
    projected = jnp.dot(attn, out_weight, preferred_element_type=jnp.float32)
    terms = jnp.sum(piece.astype(jnp.float32) * projected, axis=0)
    gate_terms = terms
    grad_attn, gate_terms = (grad_acc, gate_terms)
    grad_heads = grad_attn.astype(jnp.bfloat16).reshape(split_shape)
    delta = jnp.sum(
        grad_heads.astype(jnp.float32) * attn.reshape(split_shape).astype(jnp.float32), axis=-1
    ).T

    def grad_block(key_block, value_block, allow_mask):
        weights = weights_for(key_block, allow_mask)
        grad_weights = jnp.einsum(
            "qhd,khd->hqk", grad_heads, value_block, preferred_element_type=jnp.float32
        )
        grad_scores = (weights * (grad_weights - delta[:, :, None])).astype(jnp.bfloat16)
        query_part = jnp.einsum(
            "hqk,khd->hqd", grad_scores, key_block, preferred_element_type=jnp.float32
        )
        key_part = (
            jnp.einsum("hqk,qhd->khd", grad_scores, queries, preferred_element_type=jnp.float32)
            * score_scale
        )
        value_part = jnp.einsum(
            "hqk,qhd->khd",
            weights.astype(jnp.bfloat16),
            grad_heads,
            preferred_element_type=jnp.float32,
        )
        return (query_part, key_part, value_part)

    text_query_part, text_key_part, text_value_part = grad_block(
        text_key_split, text_value_split, text_open
    )
    text_key_grad = text_key_part.reshape(text_count, feature_width)
    text_value_grad = text_value_part.reshape(text_count, feature_width)

    def back_step(query_acc, inputs):
        key_block, value_block, allow = inputs
        query_part, key_part, value_part = grad_block(key_block, value_block, allow[:, None, None])
        stacked = jnp.stack(
            [
                key_part.reshape(tile_rows, feature_width),
                value_part.reshape(tile_rows, feature_width),
            ]
        )
        return (query_acc + query_part, stacked)

    query_acc, partials = lax.scan(
        back_step,
        jnp.zeros((head_count, tile_rows, HEAD_DIM), jnp.float32),
        (block_keys, block_values, allow_rows),
    )
    own_total = partials[4]
    for number in range(9):
        if number != 4:
            own_total = own_total + from_behind(
                partials[number].astype(jnp.bfloat16),
                "seq",
                -(int(row_steps[number]) * COLS + int(col_steps[number])),
            ).astype(jnp.float32)
    query_acc = query_acc + text_query_part
    text_key_sum, text_value_sum, gate_part = lax.psum(
        (text_key_grad, text_value_grad, gate_terms), "seq"
    )
    grad_gate = lax.psum(gate_part, "head")
    grad_query = (
        rotate((query_acc * score_scale).transpose(1, 0, 2), frame_pos, row_pos, col_pos, -1.0)
        .astype(jnp.bfloat16)
        .reshape(tile_rows, feature_width)
    )
    grad_key = (
        rotate(own_total[0].reshape(split_shape), frame_pos, row_pos, col_pos, -1.0)
        .astype(jnp.bfloat16)
        .reshape(tile_rows, feature_width)
    )
    grad_value = own_total[1].astype(jnp.bfloat16)
    return (
        grad_query,
        grad_key,
        grad_value,
        text_key_sum.astype(jnp.bfloat16),
        text_value_sum.astype(jnp.bfloat16),
        grad_gate,
    )


def solution(mesh):
    placed = (
        P("seq", "head"),
        P("seq", "head"),
        P("seq", "head"),
        P(None, "head"),
        P(None, "head"),
        P(),
        P("head", None),
        P(),
        P("head", None),
        P(),
        P("seq", "head"),
    )
    return jax.shard_map(
        on_device,
        mesh=mesh,
        in_specs=placed,
        out_specs=(
            P("seq", "head"),
            P("seq", "head"),
            P("seq", "head"),
            P(None, "head"),
            P(None, "head"),
            P(),
        ),
        check_vma=False,
    )
```

profile of v0, /device:TPU:0, one launch (start us, length us, event | category | flops | bytes accessed | tf_op | source)
XLA Modules:
  0.0 387.8 jit_solution(13709937597845558033)
XLA Ops:
  25.0 2.4 broadcast_multiply_fusion
  33.4 6.7 %collective-permute-start.6 = (bf16[2,384,256]{1,2,0:T(8,128)(2,1)}, bf16[2,384,256]{1,2,0:T(8,128)(2,1)}, u32[]{:S(2)}, u32[]{:S(2)}) collective-permute-start(bf16[2,384,256]{1,2,0:T(8,128)(2,1)} %pad_maximum_fusion), channel_id=1, source_target_pairs={{0,16},{2,18},{4,20},{6,22},{8,24},{10,26},{12,28},{14,30},{1,17},... | collective-permute-start | bytes 1179656 | tf_op jit(solution)/shard_map/ppermute | solution.py:20
  40.1 4.4 %collective-permute-start.5 = (bf16[2,384,256]{1,2,0:T(8,128)(2,1)}, bf16[2,384,256]{1,2,0:T(8,128)(2,1)}, u32[]{:S(2)}, u32[]{:S(2)}) collective-permute-start(bf16[2,384,256]{1,2,0:T(8,128)(2,1)} %pad_maximum_fusion), channel_id=1, source_target_pairs={{0,14},{2,16},{4,18},{6,20},{8,22},{10,24},{12,26},{14,28},{16,30}... | collective-permute-start | bytes 1179656 | tf_op jit(solution)/shard_map/ppermute | solution.py:20
  57.4 2.3 fusion.73
  61.7 27.8 %collective-permute-done = bf16[2,384,256]{1,2,0:T(8,128)(2,1)} collective-permute-done((bf16[2,384,256]{1,2,0:T(8,128)(2,1)}, bf16[2,384,256]{1,2,0:T(8,128)(2,1)}, u32[]{:S(2)}, u32[]{:S(2)}) %collective-permute-start) | collective-permute-done | bytes 393248 | tf_op jit(solution)/shard_map/ppermute | solution.py:20
  94.1 7.8 %collective-permute-done.2 = bf16[2,384,256]{1,2,0:T(8,128)(2,1)S(1)} collective-permute-done((bf16[2,384,256]{1,2,0:T(8,128)(2,1)}, bf16[2,384,256]{1,2,0:T(8,128)(2,1)S(1)}, u32[]{:S(2)}, u32[]{:S(2)}) %collective-permute-start.2) | collective-permute-done | bytes 393248 | tf_op jit(solution)/shard_map/ppermute | solution.py:20
  102.0 3.1 collective-permute-start.7
  108.5 5.2 %collective-permute-done.7 = bf16[2,384,256]{1,2,0:T(8,128)(2,1)S(1)} collective-permute-done((bf16[2,384,256]{1,2,0:T(8,128)(2,1)}, bf16[2,384,256]{1,2,0:T(8,128)(2,1)S(1)}, u32[]{:S(2)}, u32[]{:S(2)}) %collective-permute-start.7) | collective-permute-done | bytes 393248 | tf_op jit(solution)/shard_map/ppermute | solution.py:20
  113.8 2.3 fusion.93
  116.1 3.8 copy.128
  119.9 3.9 copy.126
  123.7 19.8 %while.37 = (s32[]{:T(128)}, f32[2,384]{1,0:T(2,128)S(1)}, f32[2,384]{1,0:T(2,128)S(1)}, pred[9,2]{1,0:T(8,128)(4,1)}, bf16[9,384,2,128]{3,1,2,0:T(8,128)(2,1)},...) while((s32[]{:T(128)}, f32[2,384]{1,0:T(2,128)S(1)}, f32[2,384]{1,0:T(2,128)S(1)}, ...), condition=%wide.region_3.4_spmd.clone, body=%wide.region_0.3_spmd.clone.sunk | while | flops 76975872 | bytes 2792566 | solution.py:143
  143.8 29.7 %while.38 = (s32[]{:T(128)}, f32[2,384,128]{2,1,0:T(8,128)}, pred[9,2]{1,0:T(8,128)(4,1)}, bf16[9,384,2,128]{3,1,2,0:T(8,128)(2,1)}, bf16[384,2,128]{2,0,1:T(8,1...) while((s32[]{:T(128)}, f32[2,384,128]{2,1,0:T(8,128)}, ...), condition=%wide.region_7.8_spmd.clone, body=%wide.region_6.7_spmd.clone.sunk | while | flops 152371200 | bytes 1380984 | solution.py:161
  144.5 2.5 fusion.151
  147.6 2.6 fusion.151
  151.0 2.6 fusion.151
  154.3 2.6 fusion.151
  157.6 2.6 fusion.151
  160.9 2.6 fusion.151
  164.2 2.6 fusion.151
  167.6 2.6 fusion.151
  170.9 2.6 fusion.151
  175.4 2.7 fusion.53
  181.3 55.6 %while.39 = (s32[]{:T(128)}, f32[2,384,128]{2,1,0:T(8,128)S(1)}, f32[9,2,384,256]{2,3,1,0:T(8,128)}, pred[9,2]{1,0:T(8,128)(4,1)}, bf16[9,384,2,128]{3,1,2,0:T(8...) while((s32[]{:T(128)}, f32[2,384,128]{2,1,0:T(8,128)S(1)}, ...), condition=%wide.region_10.11_spmd.clone, body=%wide.region_9.10_spmd.clone.sunk | while | flops 380043264 | bytes 9836705 | solution.py:223
  236.9 3.6 convert.109
  242.3 5.3 %collective-permute-start.8 = (bf16[2,384,256]{1,2,0:T(8,128)(2,1)}, bf16[2,384,256]{1,2,0:T(8,128)(2,1)}, u32[]{:S(2)}, u32[]{:S(2)}) collective-permute-start(bf16[2,384,256]{1,2,0:T(8,128)(2,1)} %get-tuple-element.342), channel_id=1, source_target_pairs={{0,18},{2,20},{4,22},{6,24},{8,26},{10,28},{12,30},{1,19},{3,21},{... | collective-permute-start | bytes 1179656 | tf_op jit(solution)/shard_map/ppermute | solution.py:20
  255.0 2.6 fusion.45
  257.6 3.9 %collective-permute-start.11 = (bf16[2,384,256]{1,2,0:T(8,128)(2,1)}, bf16[2,384,256]{1,2,0:T(8,128)(2,1)}, u32[]{:S(2)}, u32[]{:S(2)}) collective-permute-start(bf16[2,384,256]{1,2,0:T(8,128)(2,1)} %get-tuple-element.347), channel_id=1, source_target_pairs={{0,2},{2,4},{4,6},{6,8},{8,10},{10,12},{12,14},{14,16},{16,18},{18... | collective-permute-start | bytes 1179656 | tf_op jit(solution)/shard_map/ppermute | solution.py:20
  261.5 18.5 %collective-permute-done.15 = bf16[2,384,256]{1,2,0:T(8,128)(2,1)} collective-permute-done((bf16[2,384,256]{1,2,0:T(8,128)(2,1)}, bf16[2,384,256]{1,2,0:T(8,128)(2,1)}, u32[]{:S(2)}, u32[]{:S(2)}) %collective-permute-start.15) | collective-permute-done | bytes 393248 | tf_op jit(solution)/shard_map/ppermute | solution.py:20
  284.1 71.0 %all-reduce.2 = (bf16[256,256]{1,0:T(8,128)(2,1)}, bf16[256,256]{1,0:T(8,128)(2,1)}, f32[3072]{0:T(1024)S(1)}) all-reduce(f32[256,256]{1,0:T(8,128)S(1)} %copy.146, f32[256,256]{1,0:T(8,128)S(1)} %copy.148, f32[3072]{0:T(1024)S(1)} %fusion.45), channel_id=1, replica_groups=mesh['seq'=16,'head'=2] {'seq'}, use_global_device_ids=true, to_apply=%region_11.12 | all-reduce | flops 134144 | bytes 811008 | tf_op jit(solution)/shard_map/psum | solution.py:237
  355.1 8.7 %psum.31 = f32[3072]{0:T(1024)} all-reduce(f32[3072]{0:T(1024)S(1)} %get-tuple-element.339), channel_id=1, replica_groups=mesh['seq'=16,'head'=2] {'head'}, use_global_device_ids=true, to_apply=%region_15.16 | all-reduce | flops 3072 | bytes 24576 | tf_op jit(solution)/shard_map/psum | solution.py:240
  364.2 2.5 fusion.63
  (332 shorter events, 158.4 us)
Async XLA Ops:
  7.2 168.3 %copy-start = (bf16[256,3072]{1,0:T(8,128)(2,1)S(1)}, bf16[256,3072]{1,0:T(8,128)(2,1)}, u32[]{:S(2)}) copy-start(bf16[256,3072]{1,0:T(8,128)(2,1)} %param.27) | copy-start | bytes 4718596
  7.2 168.2 %all-gather.2.cloned.1.call-start = ((), (), s32[]{:S(2)}) async-start(), calls=%async_computation | async-start | bytes 3538944 | tf_op jit(solution)/shard_map/all_gather | solution.py:171
  15.0 12.4 %copy-start.6 = (f32[384,8]{1,0:T(8,128)}, f32[384,8]{1,0:T(8,128)S(1)}, u32[]{:S(2)}) copy-start(f32[384,8]{1,0:T(8,128)S(1)} %copy.103) | copy-start | bytes 36868
  32.3 16.8 %copy-start.39 = (s32[16,3]{0,1:T(4,128)S(1)}, s32[16,3]{0,1:T(4,128)}, u32[]{:S(2)}) copy-start(s32[16,3]{0,1:T(4,128)} %param.26) | copy-start | bytes 580
  32.3 16.9 %copy-start.43 = (s32[256]{0:T(256)S(1)}, s32[256]{0:T(256)}, u32[]{:S(2)}) copy-start(s32[256]{0:T(256)} %param.24) | copy-start | bytes 3076
  32.3 17.4 %copy-start.40 = (s32[2,2]{1,0:T(2,128)S(1)}, s32[2,2]{1,0:T(2,128)}, u32[]{:S(2)}) copy-start(s32[2,2]{1,0:T(2,128)} %param.25) | copy-start | bytes 52
  32.3 18.2 %copy-start.41 = (s32[9]{0:T(128)S(1)}, s32[9]{0:T(128)}, u32[]{:S(2)}) copy-start(s32[9]{0:T(128)} %constant.163) | copy-start | bytes 112
  32.4 18.2 %copy-start.42 = (s32[9]{0:T(128)S(1)}, s32[9]{0:T(128)}, u32[]{:S(2)}) copy-start(s32[9]{0:T(128)} %constant.162) | copy-start | bytes 112
  32.4 18.8 %copy-start.30 = (bf16[256,256]{1,0:T(8,128)(2,1)S(1)}, bf16[256,256]{1,0:T(8,128)(2,1)}, u32[]{:S(2)}) copy-start(bf16[256,256]{1,0:T(8,128)(2,1)} %param.22) | copy-start | bytes 393220
  32.4 19.5 %copy-start.34 = (f32[384,8]{0,1:T(8,128)S(1)}, f32[384,8]{0,1:T(8,128)}, u32[]{:S(2)}) copy-start(f32[384,8]{0,1:T(8,128)} %get-tuple-element.414) | copy-start | bytes 36868
  32.6 20.1 %copy-start.4 = (bf16[384,2,128]{0,2,1:T(8,128)(2,1)}, bf16[384,2,128]{0,2,1:T(8,128)(2,1)S(1)}, u32[]{:S(2)}) copy-start(bf16[384,2,128]{0,2,1:T(8,128)(2,1)S(1)} %copy.110) | copy-start | bytes 589828
  33.4 74.1 %collective-permute-start.6 = (bf16[2,384,256]{1,2,0:T(8,128)(2,1)}, bf16[2,384,256]{1,2,0:T(8,128)(2,1)}, u32[]{:S(2)}, u32[]{:S(2)}) collective-permute-start(bf16[2,384,256]{1,2,0:T(8,128)(2,1)} %pad_maximum_fusion), channel_id=1, source_target_pairs={{0,16},{2,18},{4,20},{6,22},{8,24},{10,26},{12,28},{14,30},{1,17},... | collective-permute-start | bytes 1179656 | tf_op jit(solution)/shard_map/ppermute | solution.py:20
  40.1 66.3 %collective-permute-start.5 = (bf16[2,384,256]{1,2,0:T(8,128)(2,1)}, bf16[2,384,256]{1,2,0:T(8,128)(2,1)}, u32[]{:S(2)}, u32[]{:S(2)}) collective-permute-start(bf16[2,384,256]{1,2,0:T(8,128)(2,1)} %pad_maximum_fusion), channel_id=1, source_target_pairs={{0,14},{2,16},{4,18},{6,20},{8,22},{10,24},{12,26},{14,28},{16,30}... | collective-permute-start | bytes 1179656 | tf_op jit(solution)/shard_map/ppermute | solution.py:20
  44.5 60.8 %collective-permute-start.4 = (bf16[2,384,256]{1,2,0:T(8,128)(2,1)}, bf16[2,384,256]{1,2,0:T(8,128)(2,1)}, u32[]{:S(2)}, u32[]{:S(2)}) collective-permute-start(bf16[2,384,256]{1,2,0:T(8,128)(2,1)} %pad_maximum_fusion), channel_id=1, source_target_pairs={{0,2},{2,4},{4,6},{6,8},{8,10},{10,12},{12,14},{14,16},{16,18},{18... | collective-permute-start | bytes 1179656 | tf_op jit(solution)/shard_map/ppermute | solution.py:20
  46.5 45.3 %collective-permute-start.1 = (bf16[2,384,256]{1,2,0:T(8,128)(2,1)}, bf16[2,384,256]{1,2,0:T(8,128)(2,1)}, u32[]{:S(2)}, u32[]{:S(2)}) collective-permute-start(bf16[2,384,256]{1,2,0:T(8,128)(2,1)} %pad_maximum_fusion), channel_id=1, source_target_pairs={{16,0},{18,2},{20,4},{22,6},{24,8},{26,10},{28,12},{30,14},{17,1},... | collective-permute-start | bytes 1179656 | tf_op jit(solution)/shard_map/ppermute | solution.py:20
  47.8 41.6 %collective-permute-start = (bf16[2,384,256]{1,2,0:T(8,128)(2,1)}, bf16[2,384,256]{1,2,0:T(8,128)(2,1)}, u32[]{:S(2)}, u32[]{:S(2)}) collective-permute-start(bf16[2,384,256]{1,2,0:T(8,128)(2,1)} %pad_maximum_fusion), channel_id=1, source_target_pairs={{18,0},{20,2},{22,4},{24,6},{26,8},{28,10},{30,12},{19,1},{21,3},{... | collective-permute-start | bytes 1179656 | tf_op jit(solution)/shard_map/ppermute | solution.py:20
  57.4 47.8 %copy-start.5 = (bf16[384,2,128]{0,2,1:T(8,128)(2,1)S(1)}, bf16[384,2,128]{0,2,1:T(8,128)(2,1)}, u32[]{:S(2)}) copy-start(bf16[384,2,128]{0,2,1:T(8,128)(2,1)} %copy-done.4) | copy-start | bytes 589828
  89.4 12.5 %collective-permute-start.2 = (bf16[2,384,256]{1,2,0:T(8,128)(2,1)}, bf16[2,384,256]{1,2,0:T(8,128)(2,1)S(1)}, u32[]{:S(2)}, u32[]{:S(2)}) collective-permute-start(bf16[2,384,256]{1,2,0:T(8,128)(2,1)} %pad_maximum_fusion), channel_id=1, source_target_pairs={{14,0},{16,2},{18,4},{20,6},{22,8},{24,10},{26,12},{28,14},{30,16}... | collective-permute-start | bytes 1179656 | tf_op jit(solution)/shard_map/ppermute | solution.py:20
  91.8 13.4 %collective-permute-start.3 = (bf16[2,384,256]{1,2,0:T(8,128)(2,1)}, bf16[2,384,256]{1,2,0:T(8,128)(2,1)S(1)}, u32[]{:S(2)}, u32[]{:S(2)}) collective-permute-start(bf16[2,384,256]{1,2,0:T(8,128)(2,1)} %pad_maximum_fusion), channel_id=1, source_target_pairs={{2,0},{4,2},{6,4},{8,6},{10,8},{12,10},{14,12},{16,14},{18,16},{20... | collective-permute-start | bytes 1179656 | tf_op jit(solution)/shard_map/ppermute | solution.py:20
  102.0 11.7 %collective-permute-start.7 = (bf16[2,384,256]{1,2,0:T(8,128)(2,1)}, bf16[2,384,256]{1,2,0:T(8,128)(2,1)S(1)}, u32[]{:S(2)}, u32[]{:S(2)}) collective-permute-start(bf16[2,384,256]{1,2,0:T(8,128)(2,1)} %pad_maximum_fusion), channel_id=1, source_target_pairs={{0,18},{2,20},{4,22},{6,24},{8,26},{10,28},{12,30},{1,19},{3,21},{... | collective-permute-start | bytes 1179656 | tf_op jit(solution)/shard_map/ppermute | solution.py:20
  123.7 19.8 %copy-start.37 = (f32[2,384]{1,0:T(2,128)S(1)}, f32[2,384]{1,0:T(2,128)}, u32[]{:S(2)}) copy-start(f32[2,384]{1,0:T(2,128)} %get-tuple-element.423) | copy-start | bytes 9220
  123.7 19.8 %copy-start.35 = (pred[256]{0:T(512)(128)(4,1)S(1)}, pred[256]{0:T(512)(128)(4,1)}, u32[]{:S(2)}) copy-start(pred[256]{0:T(512)(128)(4,1)} %broadcast_compare_fusion) | copy-start | bytes 772
  240.5 10.7 %copy-start.22 = (f32[2,128,256]{2,1,0:T(8,128)S(1)}, f32[2,128,256]{2,1,0:T(8,128)}, u32[]{:S(2)}) copy-start(f32[2,128,256]{2,1,0:T(8,128)} %fusion.89) | copy-start | bytes 786436
  242.3 15.4 %collective-permute-start.8 = (bf16[2,384,256]{1,2,0:T(8,128)(2,1)}, bf16[2,384,256]{1,2,0:T(8,128)(2,1)}, u32[]{:S(2)}, u32[]{:S(2)}) collective-permute-start(bf16[2,384,256]{1,2,0:T(8,128)(2,1)} %get-tuple-element.342), channel_id=1, source_target_pairs={{0,18},{2,20},{4,22},{6,24},{8,26},{10,28},{12,30},{1,19},{3,21},{... | collective-permute-start | bytes 1179656 | tf_op jit(solution)/shard_map/ppermute | solution.py:20
  247.6 32.4 %collective-permute-start.15 = (bf16[2,384,256]{1,2,0:T(8,128)(2,1)}, bf16[2,384,256]{1,2,0:T(8,128)(2,1)}, u32[]{:S(2)}, u32[]{:S(2)}) collective-permute-start(bf16[2,384,256]{1,2,0:T(8,128)(2,1)} %get-tuple-element.343), channel_id=1, source_target_pairs={{18,0},{20,2},{22,4},{24,6},{26,8},{28,10},{30,12},{19,1},{21,3},{... | collective-permute-start | bytes 1179656 | tf_op jit(solution)/shard_map/ppermute | solution.py:20
  248.9 33.2 %collective-permute-start.14 = (bf16[2,384,256]{1,2,0:T(8,128)(2,1)}, bf16[2,384,256]{1,2,0:T(8,128)(2,1)}, u32[]{:S(2)}, u32[]{:S(2)}) collective-permute-start(bf16[2,384,256]{1,2,0:T(8,128)(2,1)} %get-tuple-element.344), channel_id=1, source_target_pairs={{16,0},{18,2},{20,4},{22,6},{24,8},{26,10},{28,12},{30,14},{17,1},... | collective-permute-start | bytes 1179656 | tf_op jit(solution)/shard_map/ppermute | solution.py:20
  252.4 111.8 %collective-permute-start.13 = (bf16[2,384,256]{1,2,0:T(8,128)(2,1)}, bf16[2,384,256]{1,2,0:T(8,128)(2,1)}, u32[]{:S(2)}, u32[]{:S(2)}) collective-permute-start(bf16[2,384,256]{1,2,0:T(8,128)(2,1)} %get-tuple-element.345), channel_id=1, source_target_pairs={{14,0},{16,2},{18,4},{20,6},{22,8},{24,10},{26,12},{28,14},{30,16}... | collective-permute-start | bytes 1179656 | tf_op jit(solution)/shard_map/ppermute | solution.py:20
  253.7 110.5 %collective-permute-start.12 = (bf16[2,384,256]{1,2,0:T(8,128)(2,1)}, bf16[2,384,256]{1,2,0:T(8,128)(2,1)}, u32[]{:S(2)}, u32[]{:S(2)}) collective-permute-start(bf16[2,384,256]{1,2,0:T(8,128)(2,1)} %get-tuple-element.346), channel_id=1, source_target_pairs={{2,0},{4,2},{6,4},{8,6},{10,8},{12,10},{14,12},{16,14},{18,16},{20... | collective-permute-start | bytes 1179656 | tf_op jit(solution)/shard_map/ppermute | solution.py:20
  255.0 108.8 %copy-start.21 = (bf16[256,256]{0,1:T(8,128)(2,1)S(1)}, bf16[256,256]{0,1:T(8,128)(2,1)}, u32[]{:S(2)}) copy-start(bf16[256,256]{0,1:T(8,128)(2,1)} %copy.182) | copy-start | bytes 393220
  257.6 106.5 %collective-permute-start.11 = (bf16[2,384,256]{1,2,0:T(8,128)(2,1)}, bf16[2,384,256]{1,2,0:T(8,128)(2,1)}, u32[]{:S(2)}, u32[]{:S(2)}) collective-permute-start(bf16[2,384,256]{1,2,0:T(8,128)(2,1)} %get-tuple-element.347), channel_id=1, source_target_pairs={{0,2},{2,4},{4,6},{6,8},{8,10},{10,12},{12,14},{14,16},{16,18},{18... | collective-permute-start | bytes 1179656 | tf_op jit(solution)/shard_map/ppermute | solution.py:20
  280.0 84.2 %collective-permute-start.10 = (bf16[2,384,256]{1,2,0:T(8,128)(2,1)}, bf16[2,384,256]{1,2,0:T(8,128)(2,1)}, u32[]{:S(2)}, u32[]{:S(2)}) collective-permute-start(bf16[2,384,256]{1,2,0:T(8,128)(2,1)} %get-tuple-element.348), channel_id=1, source_target_pairs={{0,14},{2,16},{4,18},{6,20},{8,22},{10,24},{12,26},{14,28},{16,30}... | collective-permute-start | bytes 1179656 | tf_op jit(solution)/shard_map/ppermute | solution.py:20
  282.0 82.1 %collective-permute-start.9 = (bf16[2,384,256]{1,2,0:T(8,128)(2,1)}, bf16[2,384,256]{1,2,0:T(8,128)(2,1)}, u32[]{:S(2)}, u32[]{:S(2)}) collective-permute-start(bf16[2,384,256]{1,2,0:T(8,128)(2,1)} %get-tuple-element.349), channel_id=1, source_target_pairs={{0,16},{2,18},{4,20},{6,22},{8,24},{10,26},{12,28},{14,30},{1,17},... | collective-permute-start | bytes 1179656 | tf_op jit(solution)/shard_map/ppermute | solution.py:20
  (29 other events, 128.2 us)
Sparse Core Ops, SparseCore 0:
  49.2 37.7 all-gather.1
where the time goes:
time: 391 us; the launch traced here: 388 us
  matrix products  87.1 us (22%)
  blocking collectives  79.7 us (20%)
  local copies, waits for them, and re-layouts  71.5 us (18%)
  waiting for transfers between devices  59.3 us (15%)
  starting transfers between devices  39.8 us (10%)
  other arithmetic  32.9 us (8%)
  between operations  16.8 us (4%)
    psum x1, blocking collectives, on_device(): lax.psum((text_key_grad, text_value_grad, gate_terms), 'seq')  71 us
    ppermute x16, waiting for transfers between devices, from_behind(): return lax.ppermute(array, axis, pairs)  59.3 us
    ppermute x16, starting transfers between devices, from_behind(): return lax.ppermute(array, axis, pairs)  39.8 us
    unnamed x123, local copies, waits for them, and re-layouts  32.2 us
    dot_general x19, matrix products, head_scores(): jnp.einsum('qhd,khd->hqk', queries, key_block, preferred_element_type=jnp...  24.7 us
    dot_general x9, matrix products, output_step(): jnp.einsum('hqk,khd->hqd', probs, value_block, preferred_element_type=jnp...  23.5 us
    dot_general x10, matrix products, grad_block(): jnp.einsum('hqk,khd->hqd', grad_scores, key_block, preferred_element_type...  12.5 us
    broadcast_in_dim x18, local copies, waits for them, and re-layouts, weights_for(): return jnp.where(allow_mask, jnp.exp(scores - log_norm[:, :, None]), 0.0)  12.3 us
  transfers between devices with their start and end apart: 17, of which 4 were waited for; matrix products, arithmetic and copies ran while one was open for 22% of the time, Pallas kernels for 0%

commit v1 on v0

v1 whole, which is shorter than its diff:
```python
import functools

import jax
import jax.numpy as jnp
import numpy as np
from jax import lax
from jax.experimental import pallas as pl
from jax.experimental.pallas import tpu as pltpu
from jax.sharding import PartitionSpec as P

HEAD_DIM = 128
TILE_T = 6
TILE_H = 8
TILE_W = 8
COLS = 8
THETA = 256.0
NEG = -1e30
F32 = jnp.float32
BF16 = jnp.bfloat16


def lane_tables():
    first = HEAD_DIM // 8
    second = (HEAD_DIM - first) // 2
    freqs = np.zeros((HEAD_DIM,), np.float32)
    section = np.zeros((HEAD_DIM,), np.float32)
    sign = np.zeros((HEAD_DIM,), np.float32)
    offset = 0
    for number, length in enumerate((first, second, second)):
        half = length // 2
        f = (THETA ** (-2.0 * np.arange(half) / length)).astype(np.float32)
        freqs[offset : offset + half] = f
        freqs[offset + half : offset + length] = f
        section[offset : offset + length] = number
        sign[offset : offset + half] = -1.0
        sign[offset + half : offset + length] = 1.0
        offset += length
    return np.stack([freqs, section, sign] + [np.zeros_like(freqs)] * 5)


def partner(x):
    first = HEAD_DIM // 8
    second = (HEAD_DIM - first) // 2
    lane = lax.broadcasted_iota(jnp.int32, x.shape, 1)
    a = first // 2
    b = second // 2
    up_a = pltpu.roll(x, HEAD_DIM - a, 1)
    down_a = pltpu.roll(x, a, 1)
    up_b = pltpu.roll(x, HEAD_DIM - b, 1)
    down_b = pltpu.roll(x, b, 1)
    in_a = jnp.where(lane < a, up_a, down_a)
    is_first = (lane < first + b) | ((lane >= first + second) & (lane < first + second + b))
    in_b = jnp.where(is_first, up_b, down_b)
    return jnp.where(lane < first, in_a, in_b)


def prep_kernel(heads, tile_ref, lanes_ref, q_ref, k_ref, v_ref, qr_ref, kv_ref, cos_ref, sin_ref):
    device = lax.axis_index("seq")
    freqs = lanes_ref[0:1, :]
    section = lanes_ref[1:2, :]
    sign = lanes_ref[2:3, :]

    def table(count, base):
        step = lax.broadcasted_iota(jnp.int32, (8, HEAD_DIM), 0)
        pos = (base * count + step).astype(F32)
        angle = pos * freqs
        return jnp.cos(angle), jnp.sin(angle) * sign

    cf, sf = table(TILE_T, tile_ref[device, 0])
    cr, sr = table(TILE_H, tile_ref[device, 1])
    cc, sc = table(TILE_W, tile_ref[device, 2])
    for t in range(TILE_T):
        for r in range(TILE_H):
            at = pl.ds((t * TILE_H + r) * TILE_W, TILE_W)
            for out, f, w, c in ((cos_ref, cf, cr, cc), (sin_ref, sf, sr, sc)):
                low = jnp.where(section == 0.0, f[t : t + 1, :], w[r : r + 1, :])
                full = jnp.broadcast_to(section, c.shape)
                out[at, :] = jnp.where(full < 2.0, jnp.broadcast_to(low, c.shape), c)
    cosine = cos_ref[...]
    sine = sin_ref[...]
    for h in range(heads):
        cols = slice(h * HEAD_DIM, (h + 1) * HEAD_DIM)
        x = q_ref[:, cols].astype(F32)
        qr_ref[:, cols] = (x * cosine + partner(x) * sine).astype(BF16)
        x = k_ref[:, cols].astype(F32)
        kv_ref[0, :, cols] = (x * cosine + partner(x) * sine).astype(BF16)
    kv_ref[1] = v_ref[...]


def attend_kernel(
    deltas,
    row_count,
    reach_ref,
    mask_ref,
    q_ref,
    g_ref,
    kv_ref,
    tk_ref,
    tv_ref,
    cos_ref,
    sin_ref,
    attn_ref,
    dq_ref,
    part_ref,
    dtk_ref,
    dtv_ref,
    s_ref,
    m_ref,
    l_ref,
    o_ref,
    dqa_ref,
):
    head = pl.program_id(0)
    device = lax.axis_index("seq")
    row = device // COLS
    col = device % COLS
    tile = q_ref.shape[0]
    text = tk_ref.shape[0]
    scale = HEAD_DIM ** (-0.5)
    reach_r = reach_ref[head, 0]
    reach_c = reach_ref[head, 1]
    q = q_ref[...]
    g = g_ref[...]
    blocks = []
    for number, (dr, dc) in enumerate(deltas):
        ok = (abs(dr) <= reach_r) & (abs(dc) <= reach_c)
        ok = ok & (col + dc >= 0) & (col + dc < COLS)
        if row_count > 2:
            ok = ok & (row + dr >= 0) & (row + dr < row_count)
        blocks.append((number, ok))
    nb = len(deltas)
    text_at = slice(nb * tile, nb * tile + text)

    def nt(a, b):
        return lax.dot_general(a, b, (((1,), (1,)), ((), ())), preferred_element_type=F32)

    def tn(a, b):
        return lax.dot_general(a, b, (((0,), (0,)), ((), ())), preferred_element_type=F32)

    def nn(a, b):
        return lax.dot_general(a, b, (((1,), (0,)), ((), ())), preferred_element_type=F32)

    s = nt(tk_ref[...], q) * scale
    s = jnp.where(mask_ref[...] == 1, s, NEG)
    s_ref[text_at, :] = s
    m_ref[...] = jnp.max(s, axis=0, keepdims=True)
    for number, ok in blocks:
        at = slice(number * tile, (number + 1) * tile)

        @pl.when(ok)
        def _():
            s = nt(kv_ref[number, 0], q) * scale
            s_ref[at, :] = s
            m_ref[...] = jnp.maximum(m_ref[...], jnp.max(s, axis=0, keepdims=True))

    e = jnp.exp(s_ref[text_at, :] - m_ref[...])
    s_ref[text_at, :] = e
    l_ref[...] = jnp.sum(e, axis=0, keepdims=True)
    for number, ok in blocks:
        at = slice(number * tile, (number + 1) * tile)

        @pl.when(ok)
        def _():
            e = jnp.exp(s_ref[at, :] - m_ref[...])
            s_ref[at, :] = e
            l_ref[...] += jnp.sum(e, axis=0, keepdims=True)

    inv = 1.0 / l_ref[...]
    l_ref[...] = inv
    p = (s_ref[text_at, :] * inv).astype(BF16)
    o_ref[...] = tn(tv_ref[...], p)
    dtv_ref[...] = nn(p, g)
    for number, ok in blocks:
        at = slice(number * tile, (number + 1) * tile)

        @pl.when(ok)
        def _():
            p = (s_ref[at, :] * l_ref[...]).astype(BF16)
            o_ref[...] += tn(kv_ref[number, 1], p)
            part_ref[number, 1] = nn(p, g).astype(BF16)

        @pl.when(jnp.logical_not(ok))
        def _():
            part_ref[number] = jnp.zeros(part_ref.shape[1:], BF16)

    attn = o_ref[...].T.astype(BF16)
    attn_ref[...] = attn
    delta_rows = g.astype(F32) * attn.astype(F32)
    delta = jnp.sum(delta_rows.T, axis=0, keepdims=True)
    m_ref[...] = delta
    ds = (s_ref[text_at, :] * l_ref[...] * (nt(tv_ref[...], g) - delta)).astype(BF16)
    dqa_ref[...] = tn(tk_ref[...], ds)
    dtk_ref[...] = nn(ds, q) * scale
    for number, ok in blocks:
        at = slice(number * tile, (number + 1) * tile)

        @pl.when(ok)
        def _():
            dp = nt(kv_ref[number, 1], g)
            ds = (s_ref[at, :] * l_ref[...] * (dp - m_ref[...])).astype(BF16)
            dqa_ref[...] += tn(kv_ref[number, 0], ds)
            part_ref[number, 0] = (nn(ds, q) * scale).astype(BF16)

    dq = dqa_ref[...].T * scale
    dq_ref[...] = (dq * cos_ref[...] - partner(dq) * sin_ref[...]).astype(BF16)


def post_kernel(heads, count, *refs):
    parts = refs[:count]
    cos_ref, sin_ref, dk_ref, dv_ref = refs[count:]
    cosine = cos_ref[...]
    sine = sin_ref[...]
    for h in range(heads):
        cols = slice(h * HEAD_DIM, (h + 1) * HEAD_DIM)
        dk = parts[0][0, :, cols].astype(F32)
        dv = parts[0][1, :, cols].astype(F32)
        for part in parts[1:]:
            dk = dk + part[0, :, cols].astype(F32)
            dv = dv + part[1, :, cols].astype(F32)
        dk_ref[:, cols] = (dk * cosine - partner(dk) * sine).astype(BF16)
        dv_ref[:, cols] = dv.astype(BF16)


def shift(array, dr, dc, row_count):
    pairs = []
    for r in range(row_count):
        for c in range(COLS):
            to_r, to_c = r + dr, c + dc
            if row_count == 2:
                to_r = to_r % 2
            if 0 <= to_r < row_count and 0 <= to_c < COLS:
                pairs.append((r * COLS + c, to_r * COLS + to_c))
    return lax.ppermute(array, "seq", pairs)


def on_device(
    query_in,
    key_in,
    value_in,
    text_keys,
    text_values,
    text_mask,
    window_reach,
    tile_map,
    out_weight,
    gate_scale,
    grad_out,
):
    tile, width = query_in.shape
    heads = width // HEAD_DIM
    text = text_keys.shape[0]
    seq_count = lax.axis_size("seq")
    head_count = lax.axis_size("head")
    row_count = seq_count // COLS
    device = lax.axis_index("seq")
    mine = lax.axis_index("head")
    my_cols = grad_out.shape[1]
    vmem = pl.BlockSpec(memory_space=pltpu.VMEM)
    smem = pl.BlockSpec(memory_space=pltpu.SMEM)

    q_rot, kv, cosine, sine = pl.pallas_call(
        functools.partial(prep_kernel, heads),
        out_shape=(
            jax.ShapeDtypeStruct((tile, width), BF16),
            jax.ShapeDtypeStruct((2, tile, width), BF16),
            jax.ShapeDtypeStruct((tile, HEAD_DIM), F32),
            jax.ShapeDtypeStruct((tile, HEAD_DIM), F32),
        ),
        in_specs=[smem, vmem, vmem, vmem, vmem],
        out_specs=(vmem, vmem, vmem, vmem),
    )(tile_map, jnp.asarray(lane_tables()), query_in, key_in, value_in)

    row_deltas = (0,) if row_count == 1 else (0, 1) if row_count == 2 else (0, -1, 1)
    deltas = [(dr, dc) for dr in row_deltas for dc in (0, -1, 1)]
    by_row = {dr: kv if dr == 0 else shift(kv, -dr, 0, row_count) for dr in row_deltas}
    fetched = [by_row[dr] if dc == 0 else shift(by_row[dr], 0, -dc, row_count) for dr, dc in deltas]

    core = device % 2
    half = width // 2
    rows = [None] * head_count
    own_cols = lax.dynamic_slice_in_dim(out_weight, mine * my_cols, my_cols, 1)
    pieces = [own_cols]
    swap = [(i, i ^ 1) for i in range(seq_count)]
    for step in range(1, head_count):
        to = (mine + step) % head_count
        block = lax.dynamic_slice(out_weight, (core * half, to * my_cols), (half, my_cols))
        ring = [(i, (i + step) % head_count) for i in range(head_count)]
        got = lax.ppermute(block, "head", ring)
        other = lax.ppermute(got, "seq", swap)
        pieces.append(
            jnp.concatenate(
                [jnp.where(core == 0, got, other), jnp.where(core == 0, other, got)], axis=0
            )
        )
    grad_f = grad_out.astype(F32)
    gate_cols = lax.dynamic_slice_in_dim(gate_scale, mine * my_cols, my_cols, 0)
    grad_proj = (grad_f * gate_cols[None, :]).astype(BF16)
    total = lax.dot_general(grad_proj, pieces[0], (((1,), (1,)), ((), ())), preferred_element_type=F32)
    for step in range(1, head_count):
        part = lax.dot_general(
            grad_proj, pieces[step], (((1,), (1,)), ((), ())), preferred_element_type=F32
        ).astype(BF16)
        back = [(i, (i - step) % head_count) for i in range(head_count)]
        total = total + lax.ppermute(part, "head", back).astype(F32)
    grad_attn = total.astype(BF16)

    nb = len(deltas)
    blocks = jnp.stack(fetched)
    head_spec = pl.BlockSpec((tile, HEAD_DIM), lambda h: (0, h))
    text_spec = pl.BlockSpec((text, HEAD_DIM), lambda h: (0, h))
    block_spec = pl.BlockSpec((nb, 2, tile, HEAD_DIM), lambda h: (0, 0, 0, h))
    table_spec = pl.BlockSpec((tile, HEAD_DIM), lambda h: (0, 0))
    attn, grad_query, partials, text_key_grad, text_value_grad = pl.pallas_call(
        functools.partial(attend_kernel, deltas, row_count),
        grid=(heads,),
        out_shape=(
            jax.ShapeDtypeStruct((tile, width), BF16),
            jax.ShapeDtypeStruct((tile, width), BF16),
            jax.ShapeDtypeStruct((nb, 2, tile, width), BF16),
            jax.ShapeDtypeStruct((text, width), F32),
            jax.ShapeDtypeStruct((text, width), F32),
        ),
        in_specs=[
            smem,
            pl.BlockSpec((text, 1), lambda h: (0, 0)),
            head_spec,
            head_spec,
            block_spec,
            text_spec,
            text_spec,
            table_spec,
            table_spec,
        ],
        out_specs=(head_spec, head_spec, block_spec, text_spec, text_spec),
        scratch_shapes=[
            pltpu.VMEM((nb * tile + text, tile), F32),
            pltpu.VMEM((1, tile), F32),
            pltpu.VMEM((1, tile), F32),
            pltpu.VMEM((HEAD_DIM, tile), F32),
            pltpu.VMEM((HEAD_DIM, tile), F32),
        ],
        compiler_params=pltpu.CompilerParams(vmem_limit_bytes=48 * 1024 * 1024),
    )(
        window_reach,
        text_mask[:, None],
        q_rot,
        grad_attn,
        blocks,
        text_keys,
        text_values,
        cosine,
        sine,
    )

    projected = jnp.dot(attn, pieces[0], preferred_element_type=F32)
    for step in range(1, head_count):
        ring = [(i, (i + step) % head_count) for i in range(head_count)]
        projected = projected + jnp.dot(
            lax.ppermute(attn, "head", ring), pieces[step], preferred_element_type=F32
        )
    terms = jnp.sum(grad_f * projected, axis=0)

    arrived = []
    for number_row, dr in enumerate(row_deltas):
        own = [partials[number_row * 3]]
        for offset, dc in ((1, -1), (2, 1)):
            own.append(shift(partials[number_row * 3 + offset], 0, dc, row_count))
        if dr == 0:
            arrived.extend(own)
        else:
            summed = (own[0].astype(F32) + own[1].astype(F32) + own[2].astype(F32)).astype(BF16)
            arrived.append(shift(summed, dr, 0, row_count))
    grad_key, grad_value = pl.pallas_call(
        functools.partial(post_kernel, heads, len(arrived)),
        out_shape=(
            jax.ShapeDtypeStruct((tile, width), BF16),
            jax.ShapeDtypeStruct((tile, width), BF16),
        ),
        in_specs=[vmem] * (len(arrived) + 2),
        out_specs=(vmem, vmem),
    )(*arrived, cosine, sine)

    text_key_sum, text_value_sum, gate_part = lax.psum(
        (text_key_grad, text_value_grad, terms), "seq"
    )
    grad_gate = lax.all_gather(gate_part, "head", axis=0, tiled=True)
    return (
        grad_query,
        grad_key,
        grad_value,
        text_key_sum.astype(BF16),
        text_value_sum.astype(BF16),
        grad_gate,
    )


def solution(mesh):
    placed = (
        P("seq", "head"),
        P("seq", "head"),
        P("seq", "head"),
        P(None, "head"),
        P(None, "head"),
        P(),
        P("head", None),
        P(),
        P("head", None),
        P(),
        P("seq", "head"),
    )
    return jax.shard_map(
        on_device,
        mesh=mesh,
        in_specs=placed,
        out_specs=(
            P("seq", "head"),
            P("seq", "head"),
            P("seq", "head"),
            P(None, "head"),
            P(None, "head"),
            P(),
        ),
        check_vma=False,
    )
```

time: 391 us -> 159 us (0.41)
  matrix products: 87.1 us -> 3.49 us
  local copies, waits for them, and re-layouts: 71.5 us -> 6.71 us
  waiting for transfers between devices: 59.3 us -> 13.3 us
  other arithmetic: 32.9 us -> 0.27 us
  between operations: 16.8 us -> 1.01 us
  Pallas kernels: 0 us -> 14.5 us
    dot_general x71 -> x4, matrix products: 87.1 us -> 3.49 us  [the longest x1 2.01 us: on_device(): lax.dot_general(grad_proj, pieces[0], (((1,), (1,)), ((), ())), preferred...]
    ppermute x16 -> x14, waiting for transfers between devices: 59.3 us -> 13.3 us  [the longest x10 6.39 us: shift(): return lax.ppermute(array, 'seq', pairs)]
    unnamed x123 -> x34, local copies, waits for them, and re-layouts: 32.2 us -> 3.18 us
    broadcast_in_dim x27 -> x1, local copies, waits for them, and re-layouts: 18.6 us -> 0.8 us  [on_device(): text_mask[:, None]]
    pallas_call x0 -> x3, Pallas kernels: none -> 14.5 us  [the longest x1 9.24 us: on_device(): pl.pallas_call(functools.partial(attend_kernel, deltas, row_count), grid=...]
    another operation x6 -> x0, other arithmetic: 11.2 us -> none
    dynamic_update_slice x9 -> x0, other arithmetic: 8.49 us -> none  [on_device(): lax.scan(back_step, jnp.zeros((head_count, tile_rows, HEAD_DIM), jnp.floa...]
    psum x2 -> x1, blocking collectives: 79.7 us -> 72.3 us  [on_device(): lax.psum((text_key_grad, text_value_grad, terms), 'seq')]
  transfers between devices with their start and end apart: 17 -> 14, of which waited for: 4 -> 3; matrix products, arithmetic and copies ran while one was open for 22% -> 5% of each run, Pallas kernels for 0% -> 0%
where the time goes in v1:
time: 159 us; the launch traced here: 158 us
  blocking collectives  76.6 us (48%)
  starting transfers between devices  41.7 us (26%)
  Pallas kernels  14.5 us (9%)
  waiting for transfers between devices  13.3 us (8%)
  local copies, waits for them, and re-layouts  6.71 us (4%)
  matrix products  3.49 us (2%)
    psum x1, blocking collectives, on_device(): lax.psum((text_key_grad, text_value_grad, terms), 'seq')  72.3 us
    ppermute x10, starting transfers between devices, shift(): return lax.ppermute(array, 'seq', pairs)  29.4 us
    pallas_call x1, Pallas kernels, on_device(): pl.pallas_call(functools.partial(attend_kernel, deltas, row_count), grid=...  9.24 us
    ppermute x10, waiting for transfers between devices, shift(): return lax.ppermute(array, 'seq', pairs)  6.39 us
    ppermute x1, waiting for transfers between devices, on_device(): total = total + lax.ppermute(part, 'head', back).astype(F32)  5.36 us
    ppermute x1, starting transfers between devices, on_device(): lax.ppermute(attn, 'head', ring)  5.08 us
    all_gather x1, blocking collectives, on_device(): grad_gate = lax.all_gather(gate_part, 'head', axis=0, tiled=True)  4.37 us
    ppermute x1, starting transfers between devices, on_device(): other = lax.ppermute(got, 'seq', swap)  4.16 us
  transfers between devices with their start and end apart: 14, of which 3 were waited for; matrix products, arithmetic and copies ran while one was open for 5% of the time, Pallas kernels for 0%

profile of v1, /device:TPU:0, one launch (start us, length us, event | category | flops | bytes accessed | tf_op | source)
XLA Modules:
  0.0 157.7 jit_solution(11681345222100389041)
XLA Ops:
  0.6 1.4 copy.21.tile_ref
  2.0 2.5 %shard_map.163 = (bf16[384,256]{1,0:T(8,128)(2,1)}, bf16[2,384,256]{2,1,0:T(8,128)(2,1)}, f32[384,128]{1,0:T(8,128)}, f32[384,128]{1,0:T(8,128)}) custom-call(s32[16,3]{1,0:T(8,128)} %copy.21.tile_ref, f32[8,128]{1,0:T(8,128)} %constant.39.clone.lanes_ref, bf16[384,256]{1,0:T(8,128)(2,1)} %q_ref.1, bf16[384,256]{1,0:T(8,128)(2,1)} %k_ref.1, ...), custom_call_target="tpu_custom_call" | custom-call | tf_op jit(solution)/shard_map/pallas_call | solution.py:261
  4.5 2.5 %collective-permute-start.3 = (bf16[2,384,256]{2,1,0:T(8,128)(2,1)}, bf16[2,384,256]{2,1,0:T(8,128)(2,1)S(1)}, u32[]{:S(2)}, u32[]{:S(2)}) collective-permute-start(bf16[2,384,256]{2,1,0:T(8,128)(2,1)} %get-tuple-element.18), channel_id=1, source_target_pairs={{0,2},{2,4},{4,6},{6,8},{8,10},{10,12},{12,14},{16,18},{18,20},{20... | collective-permute-start | bytes 1179656 | tf_op jit(solution)/shard_map/ppermute | solution.py:233
  7.1 1.3 collective-permute-start.4
  8.4 3.5 %collective-permute-start.5 = (bf16[2,384,256]{2,1,0:T(8,128)(2,1)}, bf16[2,384,256]{2,1,0:T(8,128)(2,1)S(1)}, u32[]{:S(2)}, u32[]{:S(2)}) collective-permute-start(bf16[2,384,256]{2,1,0:T(8,128)(2,1)} %get-tuple-element.18), channel_id=1, source_target_pairs={{0,16},{2,18},{4,20},{6,22},{8,24},{10,26},{12,28},{14,30},{16,0},... | collective-permute-start | bytes 1179656 | tf_op jit(solution)/shard_map/ppermute | solution.py:233
  11.9 1.0 dynamic_slice.11
  12.9 1.6 collective-permute-start
  14.4 0.8 copy.22.mask_ref
  15.3 0.8 dynamic_slice.9
  16.0 2.0 %fusion.4 = f32[384,256]{1,0:T(8,128)S(1)} fusion(bf16[384,1536]{1,0:T(8,128)(2,1)} %param.22, f32[1536]{0:T(1024)S(1)} %dynamic_slice.9, bf16[256,3072]{1,0:T(8,128)(2,1)} %param.20, s32[]{:T(128)S(6)} %select_n.33), kind=kOutput, calls=%fused_computation.6 | convolution fusion | flops 303759360 | bytes 2365444 | tf_op jit(solution)/shard_map/dot_general | solution.py:298
  18.1 6.4 %collective-permute-done.5 = bf16[2,384,256]{2,1,0:T(8,128)(2,1)S(1)} collective-permute-done((bf16[2,384,256]{2,1,0:T(8,128)(2,1)}, bf16[2,384,256]{2,1,0:T(8,128)(2,1)S(1)}, u32[]{:S(2)}, u32[]{:S(2)}) %collective-permute-start.5) | collective-permute-done | bytes 393248 | tf_op jit(solution)/shard_map/ppermute | solution.py:233
  24.5 7.7 %collective-permute-start.6 = (bf16[2,384,256]{2,1,0:T(8,128)(2,1)S(1)}, bf16[2,384,256]{2,1,0:T(8,128)(2,1)S(1)}, u32[]{:S(2)}, u32[]{:S(2)}) collective-permute-start(bf16[2,384,256]{2,1,0:T(8,128)(2,1)S(1)} %collective-permute-done.5), channel_id=1, source_target_pairs={{0,2},{2,4},{4,6},{6,8},{8,10},{10,12},{12,14},{16,18},{18,20},{20... | collective-permute-start | bytes 1179656 | tf_op jit(solution)/shard_map/ppermute | solution.py:233
  32.2 1.3 collective-permute-start.7
  33.5 4.2 %collective-permute-start.1 = (bf16[128,1536]{1,0:T(8,128)(2,1)S(1)}, bf16[128,1536]{1,0:T(8,128)(2,1)S(1)}, u32[]{:S(2)}, u32[]{:S(2)}) collective-permute-start(bf16[128,1536]{1,0:T(8,128)(2,1)S(1)} %collective-permute-done), channel_id=1, source_target_pairs={{0,2},{2,0},{4,6},{6,4},{8,10},{10,8},{12,14},{14,12},{16,18},{18,... | collective-permute-start | bytes 1179656 | tf_op jit(solution)/shard_map/ppermute | solution.py:289
  37.8 1.6 collective-permute-done.1
  39.5 0.5 convolution_convert_fusion
  40.0 1.6 collective-permute-start.2
  41.7 5.4 %collective-permute-done.2 = bf16[384,256]{1,0:T(8,128)(2,1)S(1)} collective-permute-done((bf16[384,256]{1,0:T(8,128)(2,1)S(1)}, bf16[384,256]{1,0:T(8,128)(2,1)S(1)}, u32[]{:S(2)}, u32[]{:S(2)}) %collective-permute-start.2) | collective-permute-done | bytes 196640 | tf_op jit(solution)/shard_map/ppermute | solution.py:304
  47.1 9.2 %shard_map.164 = (bf16[384,256]{1,0:T(8,128)(2,1)S(1)}, bf16[384,256]{1,0:T(8,128)(2,1)}, bf16[6,2,384,256]{3,2,1,0:T(8,128)(2,1)S(1)}, f32[256,256]{1,0:T(8,128)S(1)}, f32[256,256]{1,0:T(8,128)S(1)}) custom-call(s32[2,2]{1,0:T(2,128)S(1)} %copy-done.5, s32[256,1]{1,0:T(8,128)S(1)} %copy.22.mask_ref, bf16[384,256]{1,0:T(8,128)(2,1)S(1)} %copy-done.2, ...), custom_call_target="tpu_custom_call" | custom-call | tf_op jit(solution)/shard_map/pallas_call | solution.py:313
  56.4 5.1 %collective-permute-start.13 = (bf16[384,256]{1,0:T(8,128)(2,1)S(1)}, bf16[384,256]{1,0:T(8,128)(2,1)S(1)}, u32[]{:S(2)}, u32[]{:S(2)}) collective-permute-start(bf16[384,256]{1,0:T(8,128)(2,1)S(1)} %get-tuple-element.27), channel_id=1, source_target_pairs={{0,1},{1,0},{2,3},{3,2},{4,5},{5,4},{6,7},{7,6},{8,9},{9,8},{10,11... | collective-permute-start | bytes 589832 | tf_op jit(solution)/shard_map/ppermute | solution.py:359
  61.5 0.9 slice_bitcast_fusion.1
  62.3 1.3 collective-permute-start.10
  63.6 4.1 %collective-permute-start.11 = (bf16[2,384,256]{2,1,0:T(8,128)(2,1)S(1)}, bf16[2,384,256]{2,1,0:T(8,128)(2,1)S(1)}, u32[]{:S(2)}, u32[]{:S(2)}) collective-permute-start(bf16[2,384,256]{2,1,0:T(8,128)(2,1)S(1)} %get-tuple-element.32), channel_id=1, source_target_pairs={{0,2},{2,4},{4,6},{6,8},{8,10},{10,12},{12,14},{16,18},{18,20},{20... | collective-permute-start | bytes 1179656 | tf_op jit(solution)/shard_map/ppermute | solution.py:233
  67.8 1.3 collective-permute-start.8
  69.1 5.3 %collective-permute-start.9 = (bf16[2,384,256]{2,1,0:T(8,128)(2,1)S(1)}, bf16[2,384,256]{2,1,0:T(8,128)(2,1)S(1)}, u32[]{:S(2)}, u32[]{:S(2)}) collective-permute-start(bf16[2,384,256]{2,1,0:T(8,128)(2,1)S(1)} %get-tuple-element.33), channel_id=1, source_target_pairs={{0,2},{2,4},{4,6},{6,8},{8,10},{10,12},{12,14},{16,18},{18,20},{20... | collective-permute-start | bytes 1179656 | tf_op jit(solution)/shard_map/ppermute | solution.py:233
  75.0 1.1 collective-permute-start.12
  76.1 0.5 fusion.2
  76.6 72.3 %all-reduce.2 = (bf16[256,256]{1,0:T(8,128)(2,1)}, bf16[256,256]{1,0:T(8,128)(2,1)}, f32[1536]{0:T(1024)S(1)}) all-reduce(f32[256,256]{1,0:T(8,128)S(1)} %get-tuple-element.25, f32[256,256]{1,0:T(8,128)S(1)} %get-tuple-element.26, f32[1536]{0:T(1024)S(1)} %fusion.2), channel_id=1, replica_groups=mesh['seq'=16,'head'=2] {'seq'}, use_global_device_ids=true, to_apply=%region_0.1 | all-reduce | flops 132608 | bytes 798720 | tf_op jit(solution)/shard_map/psum | solution.py:383
  148.9 4.4 %all-gather = f32[2,1,1536]{2,1,0:T(1,128)S(1)} all-gather(f32[1,1,1536]{2,1,0:T(1,128)S(1)} %reshape.16), channel_id=1, replica_groups=mesh['seq'=16,'head'=2] {'head'}, dimensions={0}, use_global_device_ids=true | all-gather | bytes 18432 | tf_op jit(solution)/shard_map/all_gather | solution.py:386
  153.3 0.7 copy-done.10
  154.3 2.7 %shard_map.165 = (bf16[384,256]{1,0:T(8,128)(2,1)}, bf16[384,256]{1,0:T(8,128)(2,1)}) custom-call(bf16[2,384,256]{2,1,0:T(8,128)(2,1)} %get-tuple-element.35.refs_0_, bf16[2,384,256]{2,1,0:T(8,128)(2,1)} %copy-done.10, bf16[2,384,256]{2,1,0:T(8,128)(2,1)} %copy-done.11, bf16[2,384,256]{2,1,0:T(8,128)(2,1)} %copy-done.12, ...), custom_call_target="tpu_custom_call" | custom-call | tf_op jit(solution)/shard_map/pallas_call | solution.py:373
  157.1 0.6 copy.34
  (47 shorter events, 1.3 us)
Async XLA Ops:
  4.5 13.5 %copy-start.9 = (bf16[2,384,256]{2,1,0:T(8,128)(2,1)S(1)}, bf16[2,384,256]{2,1,0:T(8,128)(2,1)}, u32[]{:S(2)}) copy-start(bf16[2,384,256]{2,1,0:T(8,128)(2,1)} %get-tuple-element.18) | copy-start | bytes 1179652
  4.5 33.2 %collective-permute-start.3 = (bf16[2,384,256]{2,1,0:T(8,128)(2,1)}, bf16[2,384,256]{2,1,0:T(8,128)(2,1)S(1)}, u32[]{:S(2)}, u32[]{:S(2)}) collective-permute-start(bf16[2,384,256]{2,1,0:T(8,128)(2,1)} %get-tuple-element.18), channel_id=1, source_target_pairs={{0,2},{2,4},{4,6},{6,8},{8,10},{10,12},{12,14},{16,18},{18,20},{20... | collective-permute-start | bytes 1179656 | tf_op jit(solution)/shard_map/ppermute | solution.py:233
  7.1 30.6 %collective-permute-start.4 = (bf16[2,384,256]{2,1,0:T(8,128)(2,1)}, bf16[2,384,256]{2,1,0:T(8,128)(2,1)S(1)}, u32[]{:S(2)}, u32[]{:S(2)}) collective-permute-start(bf16[2,384,256]{2,1,0:T(8,128)(2,1)} %get-tuple-element.18), channel_id=1, source_target_pairs={{2,0},{4,2},{6,4},{8,6},{10,8},{12,10},{14,12},{18,16},{20,18},{22... | collective-permute-start | bytes 1179656 | tf_op jit(solution)/shard_map/ppermute | solution.py:233
  8.4 16.1 %collective-permute-start.5 = (bf16[2,384,256]{2,1,0:T(8,128)(2,1)}, bf16[2,384,256]{2,1,0:T(8,128)(2,1)S(1)}, u32[]{:S(2)}, u32[]{:S(2)}) collective-permute-start(bf16[2,384,256]{2,1,0:T(8,128)(2,1)} %get-tuple-element.18), channel_id=1, source_target_pairs={{0,16},{2,18},{4,20},{6,22},{8,24},{10,26},{12,28},{14,30},{16,0},... | collective-permute-start | bytes 1179656 | tf_op jit(solution)/shard_map/ppermute | solution.py:233
  12.9 20.6 %collective-permute-start = (bf16[128,1536]{1,0:T(8,128)(2,1)S(1)}, bf16[128,1536]{1,0:T(8,128)(2,1)S(1)}, u32[]{:S(2)}, u32[]{:S(2)}) collective-permute-start(bf16[128,1536]{1,0:T(8,128)(2,1)S(1)} %dynamic_slice.11), channel_id=1, source_target_pairs={{0,1},{1,0},{2,3},{3,2},{4,5},{5,4},{6,7},{7,6},{8,9},{9,8},{10,11... | collective-permute-start | bytes 1179656 | tf_op jit(solution)/shard_map/ppermute | solution.py:288
  18.1 21.4 %copy-start.7 = (bf16[384,1536]{1,0:T(8,128)(2,1)S(1)}, bf16[384,1536]{1,0:T(8,128)(2,1)}, u32[]{:S(2)}) copy-start(bf16[384,1536]{1,0:T(8,128)(2,1)} %param.22) | copy-start | bytes 3538948
  24.5 17.1 %collective-permute-start.6 = (bf16[2,384,256]{2,1,0:T(8,128)(2,1)S(1)}, bf16[2,384,256]{2,1,0:T(8,128)(2,1)S(1)}, u32[]{:S(2)}, u32[]{:S(2)}) collective-permute-start(bf16[2,384,256]{2,1,0:T(8,128)(2,1)S(1)} %collective-permute-done.5), channel_id=1, source_target_pairs={{0,2},{2,4},{4,6},{6,8},{8,10},{10,12},{12,14},{16,18},{18,20},{20... | collective-permute-start | bytes 1179656 | tf_op jit(solution)/shard_map/ppermute | solution.py:233
  32.2 9.4 %collective-permute-start.7 = (bf16[2,384,256]{2,1,0:T(8,128)(2,1)S(1)}, bf16[2,384,256]{2,1,0:T(8,128)(2,1)S(1)}, u32[]{:S(2)}, u32[]{:S(2)}) collective-permute-start(bf16[2,384,256]{2,1,0:T(8,128)(2,1)S(1)} %collective-permute-done.5), channel_id=1, source_target_pairs={{2,0},{4,2},{6,4},{8,6},{10,8},{12,10},{14,12},{18,16},{20,18},{22... | collective-permute-start | bytes 1179656 | tf_op jit(solution)/shard_map/ppermute | solution.py:233
  33.5 5.8 %collective-permute-start.1 = (bf16[128,1536]{1,0:T(8,128)(2,1)S(1)}, bf16[128,1536]{1,0:T(8,128)(2,1)S(1)}, u32[]{:S(2)}, u32[]{:S(2)}) collective-permute-start(bf16[128,1536]{1,0:T(8,128)(2,1)S(1)} %collective-permute-done), channel_id=1, source_target_pairs={{0,2},{2,0},{4,6},{6,4},{8,10},{10,8},{12,14},{14,12},{16,18},{18,... | collective-permute-start | bytes 1179656 | tf_op jit(solution)/shard_map/ppermute | solution.py:289
  39.4 7.7 %copy-start = (f32[384,128]{1,0:T(8,128)S(1)}, f32[384,128]{1,0:T(8,128)}, u32[]{:S(2)}) copy-start(f32[384,128]{1,0:T(8,128)} %get-tuple-element.19.cos_ref.refs_4_) | copy-start | bytes 589828
  39.4 7.7 %copy-start.1 = (f32[384,128]{1,0:T(8,128)S(1)}, f32[384,128]{1,0:T(8,128)}, u32[]{:S(2)}) copy-start(f32[384,128]{1,0:T(8,128)} %get-tuple-element.20.sin_ref.refs_5_) | copy-start | bytes 589828
  39.5 7.7 %copy-start.2 = (bf16[384,256]{1,0:T(8,128)(2,1)S(1)}, bf16[384,256]{1,0:T(8,128)(2,1)}, u32[]{:S(2)}) copy-start(bf16[384,256]{1,0:T(8,128)(2,1)} %get-tuple-element.17.q_ref) | copy-start | bytes 589828
  39.5 7.6 %copy-start.3 = (bf16[256,256]{1,0:T(8,128)(2,1)S(1)}, bf16[256,256]{1,0:T(8,128)(2,1)}, u32[]{:S(2)}) copy-start(bf16[256,256]{1,0:T(8,128)(2,1)} %tk_ref.1) | copy-start | bytes 393220
  39.5 7.6 %copy-start.4 = (bf16[256,256]{1,0:T(8,128)(2,1)S(1)}, bf16[256,256]{1,0:T(8,128)(2,1)}, u32[]{:S(2)}) copy-start(bf16[256,256]{1,0:T(8,128)(2,1)} %tv_ref.1) | copy-start | bytes 393220
  39.5 7.6 %copy-start.5 = (s32[2,2]{1,0:T(2,128)S(1)}, s32[2,2]{1,0:T(2,128)}, u32[]{:S(2)}) copy-start(s32[2,2]{1,0:T(2,128)} %reach_ref.1) | copy-start | bytes 52
  40.0 7.0 %collective-permute-start.2 = (bf16[384,256]{1,0:T(8,128)(2,1)S(1)}, bf16[384,256]{1,0:T(8,128)(2,1)S(1)}, u32[]{:S(2)}, u32[]{:S(2)}) collective-permute-start(bf16[384,256]{1,0:T(8,128)(2,1)S(1)} %convolution_convert_fusion), channel_id=1, source_target_pairs={{0,1},{1,0},{2,3},{3,2},{4,5},{5,4},{6,7},{7,6},{8,9},{9,8},{10,11... | collective-permute-start | bytes 589832 | tf_op jit(solution)/shard_map/ppermute | solution.py:304
  41.6 5.4 %copy-start.6 = (bf16[6,2,384,256]{3,2,1,0:T(8,128)(2,1)}, bf16[6,2,384,256]{3,2,1,0:T(8,128)(2,1)S(1)}, u32[]{:S(2)}) copy-start(bf16[6,2,384,256]{3,2,1,0:T(8,128)(2,1)S(1)} %bitcast_dynamic-update-slice_fusion.kv_ref) | copy-start | bytes 7077892
  56.4 18.0 %collective-permute-start.13 = (bf16[384,256]{1,0:T(8,128)(2,1)S(1)}, bf16[384,256]{1,0:T(8,128)(2,1)S(1)}, u32[]{:S(2)}, u32[]{:S(2)}) collective-permute-start(bf16[384,256]{1,0:T(8,128)(2,1)S(1)} %get-tuple-element.27), channel_id=1, source_target_pairs={{0,1},{1,0},{2,3},{3,2},{4,5},{5,4},{6,7},{7,6},{8,9},{9,8},{10,11... | collective-permute-start | bytes 589832 | tf_op jit(solution)/shard_map/ppermute | solution.py:359
  62.3 12.5 %collective-permute-start.10 = (bf16[2,384,256]{2,1,0:T(8,128)(2,1)S(1)}, bf16[2,384,256]{2,1,0:T(8,128)(2,1)S(1)}, u32[]{:S(2)}, u32[]{:S(2)}) collective-permute-start(bf16[2,384,256]{2,1,0:T(8,128)(2,1)S(1)} %get-tuple-element.31), channel_id=1, source_target_pairs={{2,0},{4,2},{6,4},{8,6},{10,8},{12,10},{14,12},{18,16},{20,18},{22... | collective-permute-start | bytes 1179656 | tf_op jit(solution)/shard_map/ppermute | solution.py:233
  63.6 11.2 %collective-permute-start.11 = (bf16[2,384,256]{2,1,0:T(8,128)(2,1)S(1)}, bf16[2,384,256]{2,1,0:T(8,128)(2,1)S(1)}, u32[]{:S(2)}, u32[]{:S(2)}) collective-permute-start(bf16[2,384,256]{2,1,0:T(8,128)(2,1)S(1)} %get-tuple-element.32), channel_id=1, source_target_pairs={{0,2},{2,4},{4,6},{6,8},{8,10},{10,12},{12,14},{16,18},{18,20},{20... | collective-permute-start | bytes 1179656 | tf_op jit(solution)/shard_map/ppermute | solution.py:233
  67.8 85.5 %collective-permute-start.8 = (bf16[2,384,256]{2,1,0:T(8,128)(2,1)S(1)}, bf16[2,384,256]{2,1,0:T(8,128)(2,1)S(1)}, u32[]{:S(2)}, u32[]{:S(2)}) collective-permute-start(bf16[2,384,256]{2,1,0:T(8,128)(2,1)S(1)} %get-tuple-element.34), channel_id=1, source_target_pairs={{2,0},{4,2},{6,4},{8,6},{10,8},{12,10},{14,12},{18,16},{20,18},{22... | collective-permute-start | bytes 1179656 | tf_op jit(solution)/shard_map/ppermute | solution.py:233
  69.1 7.0 %copy-start.8 = (bf16[256,3072]{1,0:T(8,128)(2,1)S(1)}, bf16[256,3072]{1,0:T(8,128)(2,1)}, u32[]{:S(2)}) copy-start(bf16[256,3072]{1,0:T(8,128)(2,1)} %param.20) | copy-start | bytes 4718596
  69.1 84.2 %collective-permute-start.9 = (bf16[2,384,256]{2,1,0:T(8,128)(2,1)S(1)}, bf16[2,384,256]{2,1,0:T(8,128)(2,1)S(1)}, u32[]{:S(2)}, u32[]{:S(2)}) collective-permute-start(bf16[2,384,256]{2,1,0:T(8,128)(2,1)S(1)} %get-tuple-element.33), channel_id=1, source_target_pairs={{0,2},{2,4},{4,6},{6,8},{8,10},{10,12},{12,14},{16,18},{18,20},{20... | collective-permute-start | bytes 1179656 | tf_op jit(solution)/shard_map/ppermute | solution.py:233
  75.0 78.2 %collective-permute-start.12 = (bf16[2,384,256]{2,1,0:T(8,128)(2,1)S(1)}, bf16[2,384,256]{2,1,0:T(8,128)(2,1)S(1)}, u32[]{:S(2)}, u32[]{:S(2)}) collective-permute-start(bf16[2,384,256]{2,1,0:T(8,128)(2,1)S(1)} %fusion.7), channel_id=1, source_target_pairs={{0,16},{2,18},{4,20},{6,22},{8,24},{10,26},{12,28},{14,30},{16,0},... | collective-permute-start | bytes 1179656 | tf_op jit(solution)/shard_map/ppermute | solution.py:233
  153.2 0.7 copy-start.10
  153.3 0.9 copy-start.11
  153.3 1.0 copy-start.12

commit v2 on v1

v2 whole, which is shorter than its diff:
```python
import functools

import jax
import jax.numpy as jnp
import numpy as np
from jax import lax
from jax.experimental import pallas as pl
from jax.experimental.pallas import tpu as pltpu
from jax.sharding import PartitionSpec as P

HEAD_DIM = 128
TILE_T = 6
TILE_H = 8
TILE_W = 8
COLS = 8
THETA = 256.0
NEG = -1e30
F32 = jnp.float32
BF16 = jnp.bfloat16
MESH = pl.DeviceIdType.MESH


def lane_tables():
    first = HEAD_DIM // 8
    second = (HEAD_DIM - first) // 2
    freqs = np.zeros((HEAD_DIM,), np.float32)
    section = np.zeros((HEAD_DIM,), np.float32)
    sign = np.zeros((HEAD_DIM,), np.float32)
    offset = 0
    for number, length in enumerate((first, second, second)):
        half = length // 2
        f = (THETA ** (-2.0 * np.arange(half) / length)).astype(np.float32)
        freqs[offset : offset + half] = f
        freqs[offset + half : offset + length] = f
        section[offset : offset + length] = number
        sign[offset : offset + half] = -1.0
        sign[offset + half : offset + length] = 1.0
        offset += length
    return np.stack([freqs, section, sign] + [np.zeros_like(freqs)] * 5)


def partner(x):
    first = HEAD_DIM // 8
    second = (HEAD_DIM - first) // 2
    lane = lax.broadcasted_iota(jnp.int32, x.shape, 1)
    a = first // 2
    b = second // 2
    up_a = pltpu.roll(x, HEAD_DIM - a, 1)
    down_a = pltpu.roll(x, a, 1)
    up_b = pltpu.roll(x, HEAD_DIM - b, 1)
    down_b = pltpu.roll(x, b, 1)
    in_a = jnp.where(lane < a, up_a, down_a)
    is_first = (lane < first + b) | ((lane >= first + second) & (lane < first + second + b))
    in_b = jnp.where(is_first, up_b, down_b)
    return jnp.where(lane < first, in_a, in_b)


def neighbour(row, col, dr, dc, row_count):
    to_r, to_c = row + dr, col + dc
    ok = (to_c >= 0) & (to_c < COLS)
    if row_count == 2:
        to_r = (to_r + 2) % 2
    else:
        ok = ok & (to_r >= 0) & (to_r < row_count)
    return to_r * COLS + to_c, ok


def greet(axis_devices):
    barrier = pltpu.get_barrier_semaphore()
    for target, ok in axis_devices:
        if ok is None:
            pl.semaphore_signal(barrier, inc=1, device_id=target, device_id_type=MESH)
        else:

            @pl.when(ok)
            def _():
                pl.semaphore_signal(barrier, inc=1, device_id=target, device_id_type=MESH)

    count = 0
    for _, ok in axis_devices:
        count = count + (1 if ok is None else ok.astype(jnp.int32))
    pl.semaphore_wait(barrier, count)


def guarded(ok, act):
    if ok is None:
        act()
    else:
        pl.when(ok)(act)


def mega_kernel(row_deltas, row_count, seq_count, head_count, names, *refs):
    r = dict(zip(names, refs))
    kv_ref, qr_ref, ga_ref, wall_ref = r["kv"], r["qr"], r["ga"], r["wall"]
    part_ref, attn_ref = r["part"], r["attn"]
    s_ref, m_ref, l_ref, o_ref, dqa_ref = r["s"], r["m"], r["l"], r["o"], r["dqa"]
    acc = r["acc"]
    heads = kv_ref.shape[0]
    tile, width = qr_ref.shape
    text = r["tk"].shape[0]
    half = width // 2
    my_cols = wall_ref.shape[2]
    scale = HEAD_DIM ** (-0.5)
    device = lax.axis_index("seq")
    mine = lax.axis_index("head")
    row = device // COLS
    col = device % COLS
    core = device % 2
    bits = seq_count.bit_length() - 1
    seg = 2 * text // seq_count
    per = text // seg
    far_rows = [dr for dr in row_deltas if dr != 0]
    deltas = [(dr, dc) for dr in row_deltas for dc in (0, -1, 1)]
    nb = len(deltas)

    def seq_id(index):
        return (index, mine)

    def head_id(index):
        return (device, index)

    def part_of(h):
        return slice(h * HEAD_DIM, (h + 1) * HEAD_DIM)

    col_to = {dc: neighbour(row, col, 0, dc, row_count if row_count == 2 else 1 << 20) for dc in (-1, 1)}
    row_to = {}
    for dr in far_rows:
        index, ok = neighbour(row, col, dr, 0, row_count)
        row_to[dr] = (index, None if row_count == 2 else ok)
    opposite = {dr: (dr if row_count == 2 else -dr) for dr in far_rows}
    peers = [(mine + step) % head_count for step in range(1, head_count)]
    partner_at = []
    bit_at = []
    for b in range(bits):
        bit = (device // (1 << b)) % 2
        bit_at.append(bit)
        partner_at.append(device + (1 - 2 * bit) * (1 << b))
    sibling = partner_at[0]

    loads = {}
    own_at = pl.ds(pl.multiple_of(mine * my_cols, 128), my_cols)
    wanted = [
        ("k", r["k_hbm"], r["k"]),
        ("lanes", r["lanes_hbm"], r["lanes"]),
        ("q", r["q_hbm"], r["q"]),
        ("v", r["v_hbm"], r["v"]),
        ("grad", r["grad_hbm"], r["grad"]),
        ("gate", r["gate_hbm"].at[:, own_at], r["gate"]),
        ("w", r["w_hbm"].at[:, own_at], wall_ref.at[0]),
        ("tk", r["tk_hbm"], r["tk"]),
        ("tv", r["tv_hbm"], r["tv"]),
        ("mask", r["mask_hbm"], r["mask"]),
    ]
    for i, (name, src, dst) in enumerate(wanted):
        loads[name] = pltpu.make_async_copy(src, dst, r["load_s"].at[i])
        loads[name].start()

    friends = [(seq_id(col_to[dc][0]), col_to[dc][1]) for dc in (-1, 1)]
    friends += [(seq_id(row_to[dr][0]), row_to[dr][1]) for dr in far_rows]
    friends += [(seq_id(p), None) for p in partner_at]
    friends += [(head_id(p), None) for p in peers]
    greet(friends)

    sent = []

    def start(src, dst, ss, rs, target, ok=None):
        copy = pltpu.make_async_remote_copy(
            src_ref=src, dst_ref=dst, send_sem=ss, recv_sem=rs, device_id=target, device_id_type=MESH
        )
        guarded(ok, copy.start)
        sent.append((copy, ok))
        return copy

    row_copies = {}
    col_copies = {}

    def send_rows(src, h, k):
        for dr in far_rows:
            slot = row_deltas.index(opposite[dr])
            target, ok = row_to[dr]
            row_copies[slot, h, k] = start(
                src, kv_ref.at[h, slot * 3, k], r["row_ss"].at[slot - 1, h, k],
                r["row_rs"].at[slot - 1, h, k], seq_id(target), ok,
            )

    def send_cols(src, ri, h, k, have):
        for side, dc in ((0, -1), (1, 1)):
            target, ok = col_to[dc]
            number = ri * 3 + (2 if dc == -1 else 1)
            if have is not None:
                ok = ok & have
            col_copies[side, ri, h, k] = start(
                src, kv_ref.at[h, number, k], r["col_ss"].at[side, ri, h, k],
                r["col_rs"].at[side, ri, h, k], seq_id(target), ok,
            )

    rows_at = pl.ds(pl.multiple_of(core * half, half), half)
    w_copies = []

    def send_values(h):
        send_rows(r["v_hbm"].at[:, part_of(h)], h, 1)
        if h == 0:
            for step in range(1, head_count):
                cols_at = pl.ds(pl.multiple_of(peers[step - 1] * my_cols, 128), my_cols)
                w_copies.append(
                    start(
                        r["w_hbm"].at[rows_at, cols_at], wall_ref.at[step, rows_at, :],
                        r["w_ss"].at[step - 1], r["w_rs"].at[step - 1], head_id(peers[step - 1]),
                    )
                )
        send_cols(r["v_hbm"].at[:, part_of(h)], 0, h, 1, None)

    send_values(0)
    loads["lanes"].wait()
    freqs = r["lanes"][0:1, :]
    section = r["lanes"][1:2, :]
    sign = r["lanes"][2:3, :]
    cos_ref, sin_ref = r["cos"], r["sin"]

    def table(count, base):
        step = lax.broadcasted_iota(jnp.int32, (8, HEAD_DIM), 0)
        pos = (base * count + step).astype(F32)
        angle = pos * freqs
        return jnp.cos(angle), jnp.sin(angle) * sign

    cf, sf = table(TILE_T, r["tile"][device, 0])
    cr, sr = table(TILE_H, r["tile"][device, 1])
    cc, sc = table(TILE_W, r["tile"][device, 2])
    for t in range(TILE_T):
        for y in range(TILE_H):
            at = pl.ds((t * TILE_H + y) * TILE_W, TILE_W)
            for out, f, w, c in ((cos_ref, cf, cr, cc), (sin_ref, sf, sr, sc)):
                low = jnp.where(section == 0.0, f[t : t + 1, :], w[y : y + 1, :])
                full = jnp.broadcast_to(section, c.shape)
                out[at, :] = jnp.where(full < 2.0, jnp.broadcast_to(low, c.shape), c)
    loads["k"].wait()
    for h in range(heads):
        x = r["k"][:, part_of(h)].astype(F32)
        kv_ref[h, 0, 0] = (x * cos_ref[...] + partner(x) * sin_ref[...]).astype(BF16)
        if h > 0:
            send_values(h)
        send_rows(kv_ref.at[h, 0, 0], h, 0)
        send_cols(kv_ref.at[h, 0, 0], 0, h, 0, None)
    loads["q"].wait()
    loads["v"].wait()
    for h in range(heads):
        x = r["q"][:, part_of(h)].astype(F32)
        qr_ref[:, part_of(h)] = (x * cos_ref[...] + partner(x) * sin_ref[...]).astype(BF16)
        kv_ref[h, 0, 1] = r["v"][:, part_of(h)]

    for name in ("grad", "gate", "w", "tk", "tv", "mask"):
        loads[name].wait()
    grad_ref, proj = r["grad"], r["proj"]
    proj[...] = (grad_ref[...].astype(F32) * r["gate"][...]).astype(BF16)

    def times(step):
        return lax.dot_general(
            proj[...], wall_ref[step], (((1,), (1,)), ((), ())), preferred_element_type=F32
        )

    r["ga32"][...] = times(0)

    def forward(h, k):
        for dr in far_rows:
            slot = row_deltas.index(dr)
            have = row_to[dr][1]
            guarded(have, row_copies[slot, h, k].wait_recv)
            send_cols(kv_ref.at[h, slot * 3, k], slot, h, k, have)

    def arrive(ri, h, k):
        for side in (0, 1):
            came = col_to[1 if side == 0 else -1][1]
            if ri > 0 and row_to[row_deltas[ri]][1] is not None:
                came = came & row_to[row_deltas[ri]][1]
            guarded(came, col_copies[side, ri, h, k].wait_recv)

    def nt(a, b):
        return lax.dot_general(a, b, (((1,), (1,)), ((), ())), preferred_element_type=F32)

    def tn(a, b):
        return lax.dot_general(a, b, (((0,), (0,)), ((), ())), preferred_element_type=F32)

    def nn(a, b):
        return lax.dot_general(a, b, (((1,), (0,)), ((), ())), preferred_element_type=F32)

    text_at = slice(nb * tile, nb * tile + text)

    def at_of(number):
        return slice(number * tile, (number + 1) * tile)

    def there(number):
        dr, dc = deltas[number]
        ok = None
        if dc != 0:
            ok = col_to[dc][1]
        if dr != 0 and row_to[dr][1] is not None:
            ok = row_to[dr][1] if ok is None else ok & row_to[dr][1]
        return ok

    def score(h, number):
        def act():
            dr, dc = deltas[number]
            s = nt(kv_ref[h, number, 0], qr_ref[:, part_of(h)]) * scale
            if (dr, dc) != (0, 0):
                gap = jnp.maximum(
                    abs(dr) - r["reach"][h, 0], abs(dc) - r["reach"][h, 1]
                )
                s = jnp.where(jnp.full((1, tile), gap, jnp.int32) <= 0, s, NEG)
            s_ref[at_of(number), :] = s
            m_ref[...] = jnp.maximum(m_ref[...], jnp.max(s, axis=0, keepdims=True))

        guarded(there(number), act)

    def near_scores(h):
        s = nt(r["tk"][:, part_of(h)], qr_ref[:, part_of(h)]) * scale
        mask = jnp.broadcast_to(r["mask"][...].astype(F32), (8, text)).T[:, 0:1]
        s = jnp.where(mask == 1.0, s, NEG)
        s_ref[text_at, :] = s
        m_ref[...] = jnp.max(s, axis=0, keepdims=True)
        score(h, 0)
        arrive(0, h, 0)
        score(h, 1)
        score(h, 2)

    def far_scores(h):
        for ri in range(1, len(row_deltas)):
            score(h, ri * 3)
        for ri in range(1, len(row_deltas)):
            arrive(ri, h, 0)
            score(h, ri * 3 + 1)
            score(h, ri * 3 + 2)

    def soften(h):
        e = jnp.exp(s_ref[text_at, :] - m_ref[...])
        s_ref[text_at, :] = e
        l_ref[...] = jnp.sum(e, axis=0, keepdims=True)
        for number in range(nb):

            def act():
                e = jnp.exp(s_ref[at_of(number), :] - m_ref[...])
                s_ref[at_of(number), :] = e
                l_ref[...] += jnp.sum(e, axis=0, keepdims=True)

            guarded(there(number), act)
        l_ref[...] = 1.0 / l_ref[...]

    def outputs(h):
        g = ga_ref[:, part_of(h)]
        p = (s_ref[text_at, :] * l_ref[...]).astype(BF16)
        o_ref[...] = tn(r["tv"][:, part_of(h)], p)
        dtv = nn(p, g)
        for i in range(per):
            acc[per + i, :, part_of(h)] = dtv[i * seg : (i + 1) * seg, :]
        for number in range(nb):
            if number % 3 == 1:
                arrive(number // 3, h, 1)

            def act():
                p = (s_ref[at_of(number), :] * l_ref[...]).astype(BF16)
                o_ref[...] += tn(kv_ref[h, number, 1], p)
                part_ref[h, number, 1] = nn(p, g).astype(BF16)

            guarded(there(number), act)
        attn = o_ref[...].T.astype(BF16)
        attn_ref[h] = attn
        product = g.astype(F32) * attn.astype(F32)
        m_ref[...] = jnp.sum(product.T, axis=0, keepdims=True)

    def grads(h, hooks):
        g = ga_ref[:, part_of(h)]
        q = qr_ref[:, part_of(h)]
        ds = s_ref[text_at, :] * l_ref[...] * (nt(r["tv"][:, part_of(h)], g) - m_ref[...])
        ds = ds.astype(BF16)
        dqa_ref[...] = tn(r["tk"][:, part_of(h)], ds)
        dtk = nn(ds, q) * scale
        for i in range(per):
            acc[i, :, part_of(h)] = dtk[i * seg : (i + 1) * seg, :]
        order = [n for n in range(nb) if n >= 3] + list(range(min(nb, 3)))
        for place, number in enumerate(order):
            if place % 2 == 0 and hooks:
                hooks.pop(0)()

            def act():
                dp = nt(kv_ref[h, number, 1], g)
                ds = (s_ref[at_of(number), :] * l_ref[...] * (dp - m_ref[...])).astype(BF16)
                dqa_ref[...] += tn(kv_ref[h, number, 0], ds)
                part_ref[h, number, 0] = (nn(ds, q) * scale).astype(BF16)

            guarded(there(number), act)
            if number % 3 == 2:
                return_cols(number // 3, h)
        while hooks:
            hooks.pop(0)()
        dq = dqa_ref[...].T * scale
        r["dq"][:, part_of(h)] = (dq * cos_ref[...] - partner(dq) * sin_ref[...]).astype(BF16)

    back_cols = {}

    def return_cols(ri, h):
        for k in (1, 0):
            for side, dc in ((0, -1), (1, 1)):
                target, ok = col_to[dc]
                have = row_to[row_deltas[ri]][1] if ri > 0 else None
                if have is not None:
                    ok = ok & have
                back_cols[ri, h, k, side] = start(
                    part_ref.at[h, ri * 3 + 1 + side, k], r["bcol_in"].at[side, ri, h, k],
                    r["bcol_ss"].at[side, ri, h, k], r["bcol_rs"].at[side, ri, h, k],
                    seq_id(target), ok,
                )

    def col_sum(ri, h, k):
        total = part_ref[h, ri * 3, k].astype(F32)
        have = row_to[row_deltas[ri]][1] if ri > 0 else None
        for side, dc in ((0, -1), (1, 1)):
            came = col_to[-dc][1]
            waits = came if have is None else came & have
            guarded(waits, back_cols[ri, h, k, side].wait_recv)
            got = r["bcol_in"][side, ri, h, k].astype(F32)
            total = total + jnp.where(came, got, 0.0)
        return total

    back_rows = {}

    def return_rows(h, k):
        for fi, dr in enumerate(far_rows):
            target, ok = row_to[dr]

            def act():
                r["brow_out"][fi, h, k] = col_sum(fi + 1, h, k).astype(BF16)

            guarded(ok, act)
            back_rows[fi, h, k] = start(
                r["brow_out"].at[fi, h, k], r["brow_in"].at[fi, h, k],
                r["brow_ss"].at[fi, h, k], r["brow_rs"].at[fi, h, k], seq_id(target), ok,
            )

    attn_copies = []

    def send_attn(h):
        for step in range(1, head_count):
            attn_copies.append(
                start(
                    attn_ref.at[h], r["attn_in"].at[step - 1, h],
                    r["attn_ss"].at[step - 1, h], r["attn_rs"].at[step - 1, h],
                    head_id(peers[step - 1]),
                )
            )

    starts = [0]
    state = []

    def halve(b):
        n = seq_count >> (b + 1)
        keep = starts[-1] + bit_at[b] * n
        give = starts[-1] + (1 - bit_at[b]) * n
        r["text_out"][pl.ds(n, n)] = acc[pl.ds(give, n)].astype(BF16)
        copy = start(
            r["text_out"].at[pl.ds(n, n)], r["text_in"].at[pl.ds(n, n)],
            r["text_ss"].at[b], r["text_rs"].at[b], seq_id(partner_at[b]),
        )
        starts.append(keep)
        state.append((copy, keep, n))

    def finish():
        copy, keep, n = state[-1]
        copy.wait_recv()
        acc[pl.ds(keep, n)] = acc[pl.ds(keep, n)] + r["text_in"][pl.ds(n, n)].astype(F32)

    def text_stage(b):
        def act():
            if b > 0:
                finish()
            halve(b)

        return act

    forward(0, 1)
    near_scores(0)
    swaps = []
    for step in range(1, head_count):
        w_copies[step - 1].wait_recv()
        swaps.append(
            start(
                wall_ref.at[step, rows_at, :], wall_ref.at[step, rows_at, :],
                r["swap_ss"].at[step - 1], r["swap_rs"].at[step - 1], seq_id(sibling),
            )
        )
    forward(0, 0)
    parts = []
    for step in range(1, head_count):
        swaps[step - 1].wait_recv()
        r["part_out"][step - 1] = times(step).astype(BF16)
        back = (mine + head_count - step) % head_count
        parts.append(
            start(
                r["part_out"].at[step - 1], r["part_in"].at[step - 1],
                r["part_ss"].at[step - 1], r["part_rs"].at[step - 1], head_id(back),
            )
        )
    far_scores(0)
    for h in range(1, heads):
        forward(h, 1)
    soften(0)
    total = r["ga32"][...]
    for step in range(1, head_count):
        parts[step - 1].wait_recv()
        total = total + r["part_in"][step - 1].astype(F32)
    ga_ref[...] = total.astype(BF16)
    outputs(0)
    send_attn(0)
    for h in range(1, heads):
        forward(h, 0)
    grads(0, [text_stage(b) for b in range(bits)] if heads == 1 else [])
    for h in range(1, heads):
        near_scores(h)
        return_rows(h - 1, 1)
        far_scores(h)
        return_rows(h - 1, 0)
        soften(h)
        outputs(h)
        send_attn(h)
        grads(h, [text_stage(b) for b in range(bits)] if h == heads - 1 else [])

    finish()
    base = starts[-1]
    text_res = r["text_res"]
    text_res[pl.ds(base, 1)] = acc[pl.ds(base, 1)].astype(BF16)

    def gather(b):
        n = seq_count >> (b + 1)
        at = starts[b + 1]
        return start(
            text_res.at[pl.ds(at, n)], text_res.at[pl.ds(at, n)],
            r["gather_ss"].at[b], r["gather_rs"].at[b], seq_id(partner_at[b]),
        )

    gathering = gather(bits - 1)
    return_rows(heads - 1, 1)
    return_rows(heads - 1, 0)

    for copy in attn_copies:
        copy.wait_recv()
    gate_acc = r["gate_acc"]
    piece = 384 if my_cols % 384 == 0 else 128
    for c in range(my_cols // piece):
        at = slice(c * piece, (c + 1) * piece)
        total = jnp.zeros((tile, piece), F32)
        for step in range(head_count):
            for h in range(heads):
                left = attn_ref[h] if step == 0 else r["attn_in"][step - 1, h]
                total = total + jnp.dot(
                    left, wall_ref[step, part_of(h), at], preferred_element_type=F32
                )
        gate_acc[:, at] = jnp.sum(grad_ref[:, at].astype(F32) * total, axis=0, keepdims=True)
    for b in range(bits):
        r["gate_out"][b] = gate_acc[...]
        copy = start(
            r["gate_out"].at[b], r["gate_in"].at[b], r["gate_ss"].at[b], r["gate_rs"].at[b],
            seq_id(partner_at[b]),
        )
        back_bit = bits - 1 - b
        gathering.wait_recv()
        if back_bit > 0:
            gathering = gather(back_bit - 1)
        copy.wait_recv()
        gate_acc[...] = gate_acc[...] + r["gate_in"][b]
    gate_all = r["gate_all"]
    gate_all[mine] = gate_acc[...]
    all_copies = []
    for step in range(1, head_count):
        all_copies.append(
            start(
                gate_acc, gate_all.at[mine], r["all_ss"].at[step - 1], r["all_rs"].at[step - 1],
                head_id(peers[step - 1]),
            )
        )
    for i in range(per):
        r["dtk"][i * seg : (i + 1) * seg, :] = text_res[i]
        r["dtv"][i * seg : (i + 1) * seg, :] = text_res[per + i]

    for h in range(heads):
        for k in (1, 0):
            total = col_sum(0, h, k)
            for fi, dr in enumerate(far_rows):
                came = row_to[opposite[dr]][1]
                guarded(came, back_rows[fi, h, k].wait_recv)
                got = r["brow_in"][fi, h, k].astype(F32)
                total = total + (got if came is None else jnp.where(came, got, 0.0))
            if k == 0:
                r["dk"][:, part_of(h)] = (
                    total * cos_ref[...] - partner(total) * sin_ref[...]
                ).astype(BF16)
            else:
                r["dv"][:, part_of(h)] = total.astype(BF16)
    for copy in all_copies:
        copy.wait_recv()
    for i in range(head_count):
        r["dgate"][:, i * my_cols : (i + 1) * my_cols] = gate_all[i]
    for copy, ok in sent:
        guarded(ok, copy.wait_send)


def on_device(
    query_in,
    key_in,
    value_in,
    text_keys,
    text_values,
    text_mask,
    window_reach,
    tile_map,
    out_weight,
    gate_scale,
    grad_out,
):
    tile, width = query_in.shape
    heads = width // HEAD_DIM
    text = text_keys.shape[0]
    seq_count = lax.axis_size("seq")
    head_count = lax.axis_size("head")
    row_count = seq_count // COLS
    my_cols = grad_out.shape[1]
    row_deltas = (0,) if row_count == 1 else (0, 1) if row_count == 2 else (0, -1, 1)
    nr = len(row_deltas)
    nb = 3 * nr
    nf = max(nr - 1, 1)
    peers = max(head_count - 1, 1)
    bits = seq_count.bit_length() - 1
    seg = 2 * text // seq_count
    dma = pltpu.SemaphoreType.DMA
    vmem = pl.BlockSpec(memory_space=pltpu.VMEM)
    smem = pl.BlockSpec(memory_space=pltpu.SMEM)
    hbm = pl.BlockSpec(memory_space=pl.ANY)
    lanes = lane_tables()
    inputs = [
        ("tile", tile_map, smem),
        ("reach", window_reach, smem),
        ("lanes_hbm", jnp.asarray(lanes), hbm),
        ("q_hbm", query_in, hbm),
        ("k_hbm", key_in, hbm),
        ("v_hbm", value_in, hbm),
        ("tk_hbm", text_keys, hbm),
        ("tv_hbm", text_values, hbm),
        ("mask_hbm", text_mask[None, :], hbm),
        ("w_hbm", out_weight, hbm),
        ("gate_hbm", gate_scale[None, :], hbm),
        ("grad_hbm", grad_out, hbm),
    ]
    outputs = [
        ("dq", (tile, width), BF16),
        ("dk", (tile, width), BF16),
        ("dv", (tile, width), BF16),
        ("dtk", (text, width), BF16),
        ("dtv", (text, width), BF16),
        ("dgate", (1, head_count * my_cols), F32),
    ]
    buffers = [
        ("lanes", lanes.shape, F32),
        ("q", (tile, width), BF16),
        ("k", (tile, width), BF16),
        ("v", (tile, width), BF16),
        ("tk", (text, width), BF16),
        ("tv", (text, width), BF16),
        ("mask", (1, text), jnp.int32),
        ("gate", (1, my_cols), F32),
        ("grad", (tile, my_cols), BF16),
        ("qr", (tile, width), BF16),
        ("kv", (heads, nb, 2, tile, HEAD_DIM), BF16),
        ("part", (heads, nb, 2, tile, HEAD_DIM), BF16),
        ("cos", (tile, HEAD_DIM), F32),
        ("sin", (tile, HEAD_DIM), F32),
        ("wall", (head_count, width, my_cols), BF16),
        ("ga", (tile, width), BF16),
        ("ga32", (tile, width), F32),
        ("proj", (tile, my_cols), BF16),
        ("part_out", (peers, tile, width), BF16),
        ("part_in", (peers, tile, width), BF16),
        ("attn", (heads, tile, HEAD_DIM), BF16),
        ("attn_in", (peers, heads, tile, HEAD_DIM), BF16),
        ("s", (nb * tile + text, tile), F32),
        ("m", (1, tile), F32),
        ("l", (1, tile), F32),
        ("o", (HEAD_DIM, tile), F32),
        ("dqa", (HEAD_DIM, tile), F32),
        ("bcol_in", (2, nr, heads, 2, tile, HEAD_DIM), BF16),
        ("brow_out", (nf, heads, 2, tile, HEAD_DIM), BF16),
        ("brow_in", (nf, heads, 2, tile, HEAD_DIM), BF16),
        ("acc", (seq_count, seg, width), F32),
        ("text_out", (seq_count, seg, width), BF16),
        ("text_in", (seq_count, seg, width), BF16),
        ("text_res", (seq_count, seg, width), BF16),
        ("gate_acc", (1, my_cols), F32),
        ("gate_out", (bits, 1, my_cols), F32),
        ("gate_in", (bits, 1, my_cols), F32),
        ("gate_all", (head_count, 1, my_cols), F32),
    ]
    semaphores = [("load_s", (10,))]
    for name, shape in (
        ("row", (nf, heads, 2)),
        ("col", (2, nr, heads, 2)),
        ("w", (peers,)),
        ("swap", (peers,)),
        ("part", (peers,)),
        ("attn", (peers, heads)),
        ("bcol", (2, nr, heads, 2)),
        ("brow", (nf, heads, 2)),
        ("text", (bits,)),
        ("gather", (bits,)),
        ("gate", (bits,)),
        ("all", (peers,)),
    ):
        semaphores += [(name + "_ss", shape), (name + "_rs", shape)]
    names = [entry[0] for entry in inputs + outputs + buffers + semaphores]
    results = pl.pallas_call(
        functools.partial(mega_kernel, row_deltas, row_count, seq_count, head_count, names),
        out_shape=[jax.ShapeDtypeStruct(shape, kind) for _, shape, kind in outputs],
        in_specs=[spec for _, _, spec in inputs],
        out_specs=[vmem] * len(outputs),
        scratch_shapes=[pltpu.VMEM(shape, kind) for _, shape, kind in buffers]
        + [dma(shape) for _, shape in semaphores],
        compiler_params=pltpu.CompilerParams(
            collective_id=0, has_side_effects=True, vmem_limit_bytes=60 * 1024 * 1024
        ),
    )(*[array for _, array, _ in inputs])
    return (*results[:5], results[5].reshape(-1))


def solution(mesh):
    placed = (
        P("seq", "head"),
        P("seq", "head"),
        P("seq", "head"),
        P(None, "head"),
        P(None, "head"),
        P(),
        P("head", None),
        P(),
        P("head", None),
        P(),
        P("seq", "head"),
    )
    return jax.shard_map(
        on_device,
        mesh=mesh,
        in_specs=placed,
        out_specs=(
            P("seq", "head"),
            P("seq", "head"),
            P("seq", "head"),
            P(None, "head"),
            P(None, "head"),
            P(),
        ),
        check_vma=False,
    )
```

time: 159 us -> 84.1 us (0.53)
  blocking collectives: 76.6 us -> 0 us
  Pallas kernels: 14.5 us -> 73.2 us
  starting transfers between devices: 41.7 us -> 0 us
  waiting for transfers between devices: 13.3 us -> 0 us
  matrix products: 3.49 us -> 0 us
  local copies, waits for them, and re-layouts: 6.71 us -> 9.95 us
    psum x1 -> x0, blocking collectives: 72.3 us -> none  [on_device(): lax.psum((text_key_grad, text_value_grad, terms), 'seq')]
    pallas_call x3 -> x1, Pallas kernels: 14.5 us -> 73.2 us  [on_device(): pl.pallas_call(functools.partial(mega_kernel, row_deltas, row_count, seq_...]
    ppermute x14 -> x0, starting transfers between devices: 41.7 us -> none  [the longest x10 29.4 us: shift(): return lax.ppermute(array, 'seq', pairs)]
    ppermute x14 -> x0, waiting for transfers between devices: 13.3 us -> none  [the longest x10 6.39 us: shift(): return lax.ppermute(array, 'seq', pairs)]
    unnamed x34 -> x9, local copies, waits for them, and re-layouts: 3.18 us -> 9.95 us
    all_gather x1 -> x0, blocking collectives: 4.37 us -> none  [on_device(): grad_gate = lax.all_gather(gate_part, 'head', axis=0, tiled=True)]
    dot_general x4 -> x0, matrix products: 3.49 us -> none  [the longest x1 2.01 us: on_device(): lax.dot_general(grad_proj, pieces[0], (((1,), (1,)), ((), ())), preferred...]
    dynamic_slice x2 -> x0, local copies, waits for them, and re-layouts: 1.81 us -> none  [the longest x1 1.02 us: on_device(): lax.dynamic_slice(out_weight, (core * half, to * my_cols), (half, my_cols))]
  transfers between devices with their start and end apart: 14 -> 0, of which waited for: 3 -> 0; matrix products, arithmetic and copies ran while one was open for 5% -> 0% of each run, Pallas kernels for 0% -> 0%
where the time goes in v2:
time: 84.1 us; the launch traced here: 83.8 us
  Pallas kernels  73.2 us (87%)
  local copies, waits for them, and re-layouts  9.95 us (12%)
    pallas_call x1, Pallas kernels, on_device(): pl.pallas_call(functools.partial(mega_kernel, row_deltas, row_count, seq_...  73.2 us
    unnamed x9, local copies, waits for them, and re-layouts  9.95 us

profile of v2, /device:TPU:0, one launch (start us, length us, event | category | flops | bytes accessed | tf_op | source)
XLA Modules:
  0.0 83.8 jit_solution(15549552248247946478)
XLA Ops:
  0.6 1.4 %copy.18.refs_0_ = s32[16,3]{1,0:T(8,128)} copy(s32[16,3]{0,1:T(4,128)} %param.19) | data formatting | bytes 384 | tf_op args[7]
  2.0 73.2 %shard_map.163 = (bf16[384,256]{1,0:T(8,128)(2,1)}, bf16[384,256]{1,0:T(8,128)(2,1)}, bf16[384,256]{1,0:T(8,128)(2,1)}, bf16[256,256]{1,0:T(8,128)(2,1)}, bf16[256,256]{1,0:T(8,128)(2,1)}, /*index=5*/f32[1,3072]{1,0:T(1,128)}) custom-call(s32[16,3]{1,0:T(8,128)} %copy.18.refs_0_, s32[2,2]{1,0:T(2,128)} %refs_1_.1, f32[8,128]{1,0:T(8,128)} %constant.2.clone.refs_2_, ...), custom_call_target="tpu_custom_call" | custom-call | tf_op jit(solution)/shard_map/pallas_call | solution.py:715
  75.2 0.0 copy-start
  75.3 1.6 %copy.25 = bf16[384,256]{1,0:T(8,128)(2,1)} copy(bf16[384,256]{1,0:T(8,128)(2,1)} %get-tuple-element.24) | data formatting | bytes 393216
  76.9 1.6 %copy.26 = bf16[384,256]{1,0:T(8,128)(2,1)} copy(bf16[384,256]{1,0:T(8,128)(2,1)} %get-tuple-element.25) | data formatting | bytes 393216
  78.5 1.6 %copy.27 = bf16[384,256]{1,0:T(8,128)(2,1)} copy(bf16[384,256]{1,0:T(8,128)(2,1)} %get-tuple-element.26) | data formatting | bytes 393216
  80.1 1.6 %copy.28 = bf16[256,256]{1,0:T(8,128)(2,1)} copy(bf16[256,256]{1,0:T(8,128)(2,1)} %get-tuple-element.27) | data formatting | bytes 262144
  81.7 1.6 %copy.29 = bf16[256,256]{1,0:T(8,128)(2,1)} copy(bf16[256,256]{1,0:T(8,128)(2,1)} %get-tuple-element.28) | data formatting | bytes 262144
  83.2 0.0 copy-done
  83.2 0.6 copy.30
Async XLA Ops:
  75.2 8.0 %copy-start = (f32[1,3072]{1,0:T(1,128)S(1)}, f32[1,3072]{1,0:T(1,128)}, u32[]{:S(2)}) copy-start(f32[1,3072]{1,0:T(1,128)} %get-tuple-element.17) | copy-start | bytes 36868

commit v3 on v2

--- a/solution.py
+++ b/solution.py
@@ -535,10 +535,6 @@
             r["gather_ss"].at[b], r["gather_rs"].at[b], seq_id(partner_at[b]),
         )
 
-    gathering = gather(bits - 1)
-    return_rows(heads - 1, 1)
-    return_rows(heads - 1, 0)
-
     for copy in attn_copies:
         copy.wait_recv()
     gate_acc = r["gate_acc"]
@@ -553,16 +549,17 @@
                     left, wall_ref[step, part_of(h), at], preferred_element_type=F32
                 )
         gate_acc[:, at] = jnp.sum(grad_ref[:, at].astype(F32) * total, axis=0, keepdims=True)
-    for b in range(bits):
+    for place, b in enumerate(reversed(range(bits))):
+        if place == bits - bits // 2:
+            return_rows(heads - 1, 1)
+            return_rows(heads - 1, 0)
+        gathering = gather(b)
         r["gate_out"][b] = gate_acc[...]
         copy = start(
             r["gate_out"].at[b], r["gate_in"].at[b], r["gate_ss"].at[b], r["gate_rs"].at[b],
             seq_id(partner_at[b]),
         )
-        back_bit = bits - 1 - b
         gathering.wait_recv()
-        if back_bit > 0:
-            gathering = gather(back_bit - 1)
         copy.wait_recv()
         gate_acc[...] = gate_acc[...] + r["gate_in"][b]
     gate_all = r["gate_all"]
@@ -599,6 +596,20 @@
         r["dgate"][:, i * my_cols : (i + 1) * my_cols] = gate_all[i]
     for copy, ok in sent:
         guarded(ok, copy.wait_send)
+
+
+def leave_kernel(count, *refs):
+    sources, targets, held = refs[:count], refs[count : 2 * count], refs[2 * count : 3 * count]
+    in_s, out_s = refs[3 * count :]
+    ins = [pltpu.make_async_copy(sources[i], held[i], in_s.at[i]) for i in range(count)]
+    outs = [pltpu.make_async_copy(held[i], targets[i], out_s.at[i]) for i in range(count)]
+    for copy in ins:
+        copy.start()
+    for i in range(count):
+        ins[i].wait()
+        outs[i].start()
+    for copy in outs:
+        copy.wait()
 
 
 def on_device(
@@ -723,6 +734,15 @@
             collective_id=0, has_side_effects=True, vmem_limit_bytes=60 * 1024 * 1024
         ),
     )(*[array for _, array, _ in inputs])
+    count = len(outputs)
+    results = pl.pallas_call(
+        functools.partial(leave_kernel, count),
+        out_shape=[jax.ShapeDtypeStruct(shape, kind) for _, shape, kind in outputs],
+        in_specs=[hbm] * count,
+        out_specs=[hbm] * count,
+        scratch_shapes=[pltpu.VMEM(shape, kind) for _, shape, kind in outputs]
+        + [dma((count,)), dma((count,))],
+    )(*results)
     return (*results[:5], results[5].reshape(-1))
 
 

time: 84.1 us -> 76 us (0.904)
  local copies, waits for them, and re-layouts: 9.95 us -> 1.36 us
    unnamed x9 -> x1, local copies, waits for them, and re-layouts: 9.95 us -> 1.36 us
    pallas_call x1, Pallas kernels: 73.2 us -> 71.1 us  [on_device(): pl.pallas_call(functools.partial(mega_kernel, row_deltas, row_count, seq_...]
    pallas_call x0 -> x1, Pallas kernels: none -> 2 us  [on_device(): pl.pallas_call(functools.partial(leave_kernel, count), out_shape=[jax.Sha...]
where the time goes in v3:
time: 76 us; the launch traced here: 75.3 us
  Pallas kernels  73.1 us (96%)
  local copies, waits for them, and re-layouts  1.36 us (2%)
  between operations  0.8 us (1%)
    pallas_call x1, Pallas kernels, on_device(): pl.pallas_call(functools.partial(mega_kernel, row_deltas, row_count, seq_...  71.1 us
    pallas_call x1, Pallas kernels, on_device(): pl.pallas_call(functools.partial(leave_kernel, count), out_shape=[jax.Sha...  2 us

profile of v3, /device:TPU:0, one launch (start us, length us, event | category | flops | bytes accessed | tf_op | source)
XLA Modules:
  0.0 75.3 jit_solution(10417117248879322727)
XLA Ops:
  0.6 1.4 %copy.18.refs_0_ = s32[16,3]{1,0:T(8,128)} copy(s32[16,3]{0,1:T(4,128)} %param.19) | data formatting | bytes 384 | tf_op args[7]
  2.0 71.1 %shard_map.163 = (bf16[384,256]{1,0:T(8,128)(2,1)}, bf16[384,256]{1,0:T(8,128)(2,1)}, bf16[384,256]{1,0:T(8,128)(2,1)}, bf16[256,256]{1,0:T(8,128)(2,1)}, bf16[256,256]{1,0:T(8,128)(2,1)}, /*index=5*/f32[1,3072]{1,0:T(1,128)}) custom-call(s32[16,3]{1,0:T(8,128)} %copy.18.refs_0_, s32[2,2]{1,0:T(2,128)} %refs_1_.1, f32[8,128]{1,0:T(8,128)} %constant.2.clone.refs_2_, ...), custom_call_target="tpu_custom_call" | custom-call | tf_op jit(solution)/shard_map/pallas_call | solution.py:726
  73.1 2.0 %shard_map.164 = (bf16[384,256]{1,0:T(8,128)(2,1)}, bf16[384,256]{1,0:T(8,128)(2,1)}, bf16[384,256]{1,0:T(8,128)(2,1)}, bf16[256,256]{1,0:T(8,128)(2,1)}, bf16[256,256]{1,0:T(8,128)(2,1)}, /*index=5*/f32[1,3072]{1,0:T(1,128)}) custom-call(bf16[384,256]{1,0:T(8,128)(2,1)} %get-tuple-element.18.refs_0_, bf16[384,256]{1,0:T(8,128)(2,1)} %get-tuple-element.19.refs_1_, ...), custom_call_target="tpu_custom_call" | custom-call | tf_op jit(solution)/shard_map/pallas_call | solution.py:738
